TPU v7x, 128 devices: a whole 4x4x4 slice. The times are simulated.
128 devices in a mesh: gx: 16 (over y_hi, x, core), gy: 8 (over y_lo, z).
Axes of the slice: x: 4, y: 4 (y_hi: 2, y_lo: 2; y = y_hi * 2 + y_lo), z: 4, core: 2. Of those that a mesh axis runs over, the one named last changes fastest.
Arguments:
- res_charge: float32 [262144], P(('gx', 'gy')), may hold values from -6 to 6
- res_frac: float32 [3, 262144], P(None, ('gx', 'gy')), may hold values from 0 to 1
- res_cell: int32 [262144], P(('gx', 'gy')), may hold values from 0 to 65535
- res_count: int32 [128], P(('gx', 'gy')), may hold values from 1024 to 2048, as said below
- mov_charge: float32 [65536], P(('gx', 'gy')), may hold values from -6 to 6
- mov_frac: float32 [3, 65536], P(None, ('gx', 'gy')), may hold values from 0 to 1
- mov_cell: int32 [65536], P(('gx', 'gy')), may hold values from 0 to 65535
- mov_dest: int32 [65536, 1], P(('gx', 'gy')), may hold values from 0 to 127; in each aligned block of 512 rows (0 to 511, 512 to 1023, ...) at most 8 rows name the same one
- fine_taps: float32 [3, 13], replicated, may hold values from -3 to 3
- coarse_taps: float32 [3, 13], replicated, may hold values from -3 to 3
Outputs:
- res_potential: float32 [262144], P(('gx', 'gy'))
- arrived_potential: float32 [128, 1024], P(('gx', 'gy'))
- grid_potential: float32 [512, 128, 128], P('gx', 'gy')
Inputs may be any that keep to these rules, and one draw needn't show every extreme that they name: `res_count`: a multiple of 128; some box has exactly 2048 live atoms. `mov_dest`: among the rows of one source box, at most 8 name the same destination, a bound that some block reaches of them.
All inputs are finite; a program needn't handle non-finite values.
Results may differ from a plain program's by a relative error of at most 0.0048.
Values sent between devices are 32-bit elements; how exact they have to be, the bound alone decides.
A program may use at most 64 MiB of HBM per device.

v0:
```python
import jax
import jax.numpy as jnp
from jax import lax
from jax.sharding import PartitionSpec as P

CX = 32
CY = 16
NZ = 128


def from_behind(value, axis, steps):
    count = lax.axis_size(axis)
    pairs = [(source, (source + steps) % count) for source in range(count)]
    return lax.ppermute(value, axis, pairs)


def padded_2(x, sides, width):
    for axis, dim in sides:
        size, length = (lax.axis_size(axis), x.shape[dim])
        up = [(i, (i + 1) % size) for i in range(size)]
        down = [(j, i) for i, j in up]
        last = lax.slice_in_dim(x, length - width, length, axis=dim)
        initial = lax.slice_in_dim(x, 0, width, axis=dim)
        before = lax.ppermute(last, axis, up)
        after = lax.ppermute(initial, axis, down)
        x = jnp.concatenate([before, x, after], axis=dim)
    return x


def spline_weights(fracs):
    rest = 1.0 - fracs
    cube = fracs * fracs * fracs
    square = fracs * fracs
    return jnp.stack(
        [
            rest * rest * rest / 6.0,
            (3.0 * cube - 6.0 * square + 4.0) / 6.0,
            (-3.0 * cube + 3.0 * square + 3.0 * fracs + 1.0) / 6.0,
            cube / 6.0,
        ]
    )


def stencil(first, weights, length, wrapped):
    columns = jnp.arange(length, dtype=jnp.int32)[None, :]
    result = jnp.zeros((first.shape[0], length), jnp.float32)
    for offset_k in range(4):
        where_at = first + offset_k
        if wrapped:
            where_at = where_at % length
        result = result + jnp.where(columns == where_at[:, None], weights[offset_k][:, None], 0.0)
    return result


def factors(fracs, cells):
    cell_x = cells // (CY * NZ)
    cell_y = cells // NZ % CY
    cell_z = cells % NZ
    x_weights = stencil(cell_x, spline_weights(fracs[0]), CX + 3, False)
    y_weights = stencil(cell_y, spline_weights(fracs[1]), CY + 3, False)
    z_weights = stencil(cell_z, spline_weights(fracs[2]), NZ, True)
    yz_weights = (y_weights[:, :, None] * z_weights[:, None, :]).astype(jnp.bfloat16)
    return (x_weights, yz_weights.reshape(cells.shape[0], (CY + 3) * NZ))


def blocked(charges, fracs, cells):
    rows = charges.shape[0]
    block_rows = min(512, rows)
    blocks = rows // block_rows
    return (
        charges.reshape(blocks, block_rows),
        fracs.reshape(3, blocks, block_rows).transpose(1, 0, 2),
        cells.reshape(blocks, block_rows),
    )


def spread(charges, fracs, cells):

    def advance(running, pieces):
        block_charge, block_frac, block_cell = pieces
        x_weights, yz_weights = factors(block_frac, block_cell)
        x_charge = (x_weights * block_charge[:, None]).astype(jnp.bfloat16)
        added = lax.dot_general(
            x_charge, yz_weights, (((0,), (0,)), ((), ())), preferred_element_type=jnp.float32
        )
        return (running + added, None)

    start_grid = jnp.zeros((CX + 3, (CY + 3) * NZ), jnp.float32)
    running, _ = lax.scan(advance, start_grid, blocked(charges, fracs, cells))
    return running


def sample(half_grid, charges, fracs, cells):

    def evaluate(pieces):
        block_charge, block_frac, block_cell = pieces
        x_weights, yz_weights = factors(block_frac, block_cell)
        partial_value = lax.dot_general(
            half_grid, yz_weights, (((1,), (1,)), ((), ())), preferred_element_type=jnp.float32
        )
        x_plain = lax.optimization_barrier(x_weights.astype(jnp.bfloat16)).astype(jnp.float32)
        return jnp.sum(x_plain.T * partial_value, axis=0)

    return lax.map(evaluate, blocked(charges, fracs, cells)).reshape(-1)


def along(field, filter_taps, along_dim, offset, length):
    summed = jnp.zeros(
        field.shape[:along_dim] + (length,) + field.shape[along_dim + 1 :], jnp.float32
    )
    for tap_index in range(filter_taps.shape[0]):
        summed = summed + filter_taps[tap_index] * lax.slice_in_dim(
            field, offset + tap_index, offset + tap_index + length, axis=along_dim
        )
    return summed


def beside_all(field, filter_taps):
    summed = jnp.zeros_like(field)
    half_width = filter_taps.shape[0] // 2
    for tap_index in range(filter_taps.shape[0]):
        summed = summed + filter_taps[tap_index] * jnp.roll(field, half_width - tap_index, axis=2)
    return summed


def level_field(padded, filter_taps, margin, length_x, length_y):
    half_width = filter_taps.shape[1] // 2
    field = along(padded, filter_taps[0], 0, margin - half_width, length_x)
    field = along(field, filter_taps[1], 1, margin - half_width, length_y)
    return beside_all(field, filter_taps[2])


def coarsen(field):
    size_a, size_b, size_c = field.shape
    return field.reshape(size_a // 2, 2, size_b // 2, 2, size_c // 2, 2).sum(axis=(1, 3, 5))


def on_device(
    res_charge,
    res_frac,
    res_cell,
    res_count,
    mov_charge,
    mov_frac,
    mov_cell,
    mov_dest,
    fine_taps,
    coarse_taps,
):
    count_gx = lax.axis_size("gx")
    count_gy = lax.axis_size("gy")
    devices = count_gx * count_gy
    moving = mov_charge.shape[0]
    slots = 2 * moving // devices
    targets = mov_dest[:, 0]
    hits = (targets[:, None] == jnp.arange(devices, dtype=jnp.int32)[None, :]).astype(jnp.float32)
    positions = jnp.arange(moving, dtype=jnp.int32)
    lower = (positions[:, None] >= positions[None, :]).astype(jnp.float32)
    ranks = jnp.dot(lower, hits, precision=lax.Precision.HIGHEST)
    slot = (jnp.sum(hits * ranks, axis=1) - 1.0).astype(jnp.int32)
    target_slot = targets * slots + slot
    placing = (
        target_slot[:, None] == jnp.arange(devices * slots, dtype=jnp.int32)[None, :]
    ).astype(jnp.float32)
    payload = jnp.concatenate(
        [mov_charge[None, :], mov_frac, (mov_cell.astype(jnp.float32) + 1.0)[None, :]], 0
    )
    packed = jnp.dot(payload, placing, precision=lax.Precision.HIGHEST)
    arrived = lax.all_to_all(
        packed.reshape(5, devices, slots), ("gx", "gy"), split_axis=1, concat_axis=1, tiled=True
    )
    arrived = arrived.reshape(5, devices * slots)
    live = jnp.arange(res_charge.shape[0], dtype=jnp.int32) < res_count[0]
    live_charge = jnp.where(live, res_charge, 0.0)
    resident_grid = spread(live_charge, res_frac, res_cell)
    occupied = arrived[4] > 0.5
    arrived_cell = jnp.maximum(arrived[4] - 1.0, 0.0).astype(jnp.int32)
    arrived_grid = spread(arrived[0], arrived[1:4], arrived_cell)
    extended = (resident_grid + arrived_grid).reshape(CX + 3, CY + 3, NZ)
    upper_x = from_behind(extended[CX:], "gx", 1)
    extended = extended[:CX].at[:3].add(upper_x)
    upper_y = from_behind(extended[:, CY:], "gy", 1)
    charge_grid = extended[:, :CY].at[:, :3].add(upper_y)
    fine_padded = padded_2(charge_grid, (("gx", 0), ("gy", 1)), 9)
    coarse_padded = padded_2(coarsen(charge_grid), (("gx", 0), ("gy", 1)), 8)
    fine_field = level_field(fine_padded, fine_taps, 9, CX + 3, CY + 3)
    coarse_field = level_field(coarse_padded, coarse_taps, 8, CX // 2 + 2, CY // 2 + 2)
    spread_coarse = jnp.repeat(jnp.repeat(jnp.repeat(coarse_field, 2, 0), 2, 1), 2, 2)[
        : CX + 3, : CY + 3
    ]
    field_ext = fine_field + spread_coarse
    grid_potential = field_ext[:CX, :CY]
    half_grid = field_ext.astype(jnp.bfloat16).reshape(CX + 3, (CY + 3) * NZ)
    resident_values = sample(half_grid, live_charge, res_frac, res_cell)
    arrived_values = sample(half_grid, arrived[0], arrived[1:4], arrived_cell)
    res_potential = jnp.where(live, resident_values, 0.0)
    arrived_potential = jnp.where(occupied, arrived_values, 0.0)[None, :]
    return (res_potential, arrived_potential, grid_potential)


def solution(mesh):
    return jax.shard_map(
        on_device,
        mesh=mesh,
        in_specs=(
            P(("gx", "gy")),
            P(None, ("gx", "gy")),
            P(("gx", "gy")),
            P(("gx", "gy")),
            P(("gx", "gy")),
            P(None, ("gx", "gy")),
            P(("gx", "gy")),
            P(("gx", "gy"), None),
            P(),
            P(),
        ),
        out_specs=(P(("gx", "gy")), P(("gx", "gy"), None), P("gx", "gy", None)),
        check_vma=False,
    )
```

profile of v0, /device:TPU:0, one launch (start us, length us, event | category | flops | bytes accessed | tf_op | source)
XLA Modules:
  0.0 182.6 jit_solution(335659025685137201)
XLA Ops:
  3.1 1.5 fusion.156
  5.9 11.7 %all-to-all-start = ((f32[5,128,8]{2,0,1:T(8,128)}), f32[5,128,8]{2,0,1:T(8,128)}, u32[]{:S(2)}, u32[]{:S(2)}) async-start(f32[5,128,8]{2,0,1:T(8,128)} %copy.17), calls=%async_computation | async-start | bytes 1048576 | tf_op jit(solution)/shard_map/all_to_all | solution.py:169
  19.8 9.6 %while.58 = (s32[]{:T(128)}, f32[35,2432]{1,0:T(8,128)S(1)}, s32[4,512]{1,0:T(4,128)S(1)}, f32[4,3,512]{2,1,0:T(4,128)S(1)}, f32[4,512]{1,0:T(4,128)S(1)}, /*index=5*/s32[]{:T(128)}, s32[]{:T(128)}, s32[]{}, s32[]{}) while((s32[]{:T(128)}, f32[35,2432]{1,0:T(8,128)S(1)}, s32[4,512]{1,0:T(4,128)S(1)}, f32[4,3,512]{2,1,0:T(4,128)S(1)}, ...), condition=%wide.region_1.2_spmd.clone, body=%wide.region_0.0_spmd.clone.sunk | while | flops 90961152 | bytes 6397083 | solution.py:89
  20.7 1.5 convolution_add_fusion.4
  23.1 1.5 convolution_add_fusion.4
  25.5 1.5 convolution_add_fusion.4
  34.8 4.8 %while.59 = (s32[]{:T(128)}, f32[35,2432]{1,0:T(8,128)S(1)}, s32[2,512]{1,0:T(2,128)S(1)}, f32[2,3,512]{2,1,0:T(4,128)S(1)}, f32[2,512]{1,0:T(2,128)S(1)}, /*index=5*/s32[]{:T(128)}, s32[]{:T(128)}, s32[]{}, s32[]{}) while((s32[]{:T(128)}, f32[35,2432]{1,0:T(8,128)S(1)}, s32[2,512]{1,0:T(2,128)S(1)}, f32[2,3,512]{2,1,0:T(4,128)S(1)}, ...), condition=%wide.region_4.5_spmd.clone, body=%wide.region_3.4_spmd.clone.sunk | while | flops 90961152 | bytes 6397083 | solution.py:89
  35.7 1.5 convolution_add_fusion.5
  38.1 1.5 convolution_add_fusion.5
  41.8 4.9 %collective-permute-done = f32[3,19,128]{2,1,0:T(8,128)S(1)} collective-permute-done((f32[3,19,128]{2,1,0:T(8,128)S(1)}, f32[3,19,128]{2,1,0:T(8,128)S(1)}, u32[]{:S(2)}, u32[]{:S(2)}) %collective-permute-start) | collective-permute-done | bytes 29216 | tf_op jit(solution)/shard_map/ppermute | solution.py:14
  48.6 4.6 %collective-permute-done.1 = f32[32,3,128]{2,1,0:T(4,128)S(1)} collective-permute-done((f32[32,3,128]{2,1,0:T(4,128)S(1)}, f32[32,3,128]{2,1,0:T(4,128)S(1)}, u32[]{:S(2)}, u32[]{:S(2)}) %collective-permute-start.1) | collective-permute-done | bytes 49184 | tf_op jit(solution)/shard_map/ppermute | solution.py:14
  53.5 18.1 %reshape.3264 = f32[16,2,8,2,64,2]{5,4,3,2,1,0:T(8,128)} reshape(f32[32,16,128]{2,1,0:T(8,128)S(1)} %scatter-add.9) | data formatting | bytes 524288 | tf_op jit(solution)/shard_map/reshape | solution.py:135
  71.6 7.0 %reduce_sum.45 = f32[16,8,64]{2,1,0:T(8,128)S(1)} reduce(f32[16,2,8,2,64,2]{5,4,3,2,1,0:T(8,128)} %reshape.3264, f32[]{:T(128)} %constant.878.clone.1), dimensions={1,3,5}, to_apply=%region_5.6 | reduce | flops 57344 | bytes 294916 | tf_op jit(solution)/shard_map/reduce_sum | solution.py:135
  79.2 5.0 %collective-permute-start.3 = (f32[9,16,128]{2,1,0:T(8,128)S(1)}, f32[9,16,128]{2,1,0:T(8,128)S(1)}, u32[]{:S(2)}, u32[]{:S(2)}) collective-permute-start(f32[9,16,128]{2,1,0:T(8,128)S(1)} %get-tuple-element.678), channel_id=1, source_target_pairs={{8,0},{16,8},{24,16},{32,24},{40,32},{48,40},{56,48},{64,56},{72,6... | collective-permute-start | bytes 221192 | tf_op jit(solution)/shard_map/ppermute | solution.py:25
  84.2 1.5 collective-permute-done.6
  87.9 3.8 %collective-permute-done.2 = f32[9,16,128]{2,1,0:T(8,128)S(1)} collective-permute-done((f32[9,16,128]{2,1,0:T(8,128)S(1)}, f32[9,16,128]{2,1,0:T(8,128)S(1)}, u32[]{:S(2)}, u32[]{:S(2)}) %collective-permute-start.2) | collective-permute-done | bytes 73760 | tf_op jit(solution)/shard_map/ppermute | solution.py:24
  95.3 8.3 %fusion.196 = f32[18,24,64]{2,1,0:T(8,128)S(1)} fusion(f32[32,24,64]{2,1,0:T(8,128)S(1)} %pad_maximum_fusion.2, f32[]{:T(128)} %bitcast.75, f32[]{:T(128)} %bitcast.74, f32[]{:T(128)} %bitcast.73, f32[]{:T(128)} %bitcast.72, f32[]{:T(128)} %bitcast.71, f32[]{:T(128)} %bitcast.70, f32[]{:T(128)} %bitcast.69, f32[]{:T(128)} %bitcast.68, f32[]{:T(128)} %bitcast.67, ...), kind=kLoop, calls=%fused_computation.501 | loop fusion | flops 691200 | bytes 1548340 | tf_op jit(solution)/shard_map/add | solution.py:112
  103.6 8.3 %fusion.208 = f32[18,10,64]{2,1,0:T(8,128)S(1)} fusion(f32[18,24,64]{2,1,0:T(8,128)S(1)} %fusion.196, f32[]{:T(128)} %bitcast.87, f32[]{:T(128)} %bitcast.86, f32[]{:T(128)} %bitcast.85, f32[]{:T(128)} %bitcast.84, f32[]{:T(128)} %bitcast.83, f32[]{:T(128)} %bitcast.82, f32[]{:T(128)} %bitcast.81, f32[]{:T(128)} %bitcast.80, f32[]{:T(128)} %bitcast.79, ...), kind=kLoop, calls=%fused_computation.526 | loop fusion | flops 288000 | bytes 645172 | tf_op jit(solution)/shard_map/add | solution.py:112
  113.2 17.0 %fusion.231 = f32[18,10,64]{2,1,0:T(8,128)S(1)} fusion(f32[18,10,58]{2,1,0:T(8,128)S(1)} %get-tuple-element.680, f32[18,10,6]{2,1,0:T(8,128)S(1)} %get-tuple-element.682, f32[18,10,59]{2,1,0:T(8,128)S(1)} %get-tuple-element.684, f32[18,10,5]{2,1,0:T(8,128)S(1)} %get-tuple-element.686, f32[18,10,60]{2,1,0:T(8,128)S(1)} %get-tuple-element.688, ...), kind=kLoop, calls=%fused_computation.562 | loop fusion | flops 714240 | bytes 1198184 | tf_op jit(solution)/shard_map/add | solution.py:122
  133.0 8.8 %fusion.159 = f32[35,34,128]{2,1,0:T(8,128)S(1)} fusion(f32[50,34,128]{2,1,0:T(8,128)S(1)} %pad_maximum_fusion, f32[]{:T(128)} %bitcast.36, f32[]{:T(128)} %bitcast.35, f32[]{:T(128)} %bitcast.34, f32[]{:T(128)} %bitcast.33, f32[]{:T(128)} %bitcast.32, f32[]{:T(128)} %bitcast.31, f32[]{:T(128)} %bitcast.30, f32[]{:T(128)} %bitcast.29, f32[]{:T(128)} %bitcast.28, ...), kind=kLoop, calls=%fused_computation.422 | loop fusion | flops 3808000 | bytes 8529972 | tf_op jit(solution)/shard_map/add | solution.py:112
  141.7 8.7 %fusion.171 = f32[35,19,128]{2,1,0:T(8,128)S(1)} fusion(f32[35,34,128]{2,1,0:T(8,128)S(1)} %fusion.159, f32[]{:T(128)} %bitcast.48, f32[]{:T(128)} %bitcast.47, f32[]{:T(128)} %bitcast.46, f32[]{:T(128)} %bitcast.45, f32[]{:T(128)} %bitcast.44, f32[]{:T(128)} %bitcast.43, f32[]{:T(128)} %bitcast.42, f32[]{:T(128)} %bitcast.41, f32[]{:T(128)} %bitcast.40, ...), kind=kLoop, calls=%fused_computation.447 | loop fusion | flops 2128000 | bytes 4766772 | tf_op jit(solution)/shard_map/add | solution.py:112
  152.8 18.6 %fusion.241 = (bf16[35,19,128]{2,1,0:T(8,128)(2,1)S(1)}, f32[35,19,128]{2,1,0:T(8,128)S(1)}) fusion(f32[35,19,128]{2,1,0:T(8,128)S(1)} %copy.24, f32[35,19,6]{2,1,0:T(8,128)S(1)} %get-tuple-element.650, f32[35,19,122]{2,1,0:T(8,128)S(1)} %get-tuple-element.652, f32[]{:T(128)} %bitcast.60, f32[35,19,5]{2,1,0:T(8,128)S(1)} %get-tuple-element.654, ...), kind=kLoop, calls=%fused_computation.593 | loop fusion | flops 5447680 | bytes 9363304 | tf_op jit(solution)/shard_map/convert_element_type | solution.py:193
  171.5 6.1 %while.56 = (s32[]{:T(128)}, f32[4,512]{1,0:T(4,128)S(1)}, s32[4,512]{1,0:T(4,128)S(1)}, f32[4,3,512]{2,1,0:T(4,128)S(1)}, bf16[35,2432]{1,0:T(8,128)(2,1)S(1)}, /*index=5*/s32[]{:T(128)}, s32[]{:T(128)}, s32[]{}, s32[]{}) while((s32[]{:T(128)}, f32[4,512]{1,0:T(4,128)S(1)}, s32[4,512]{1,0:T(4,128)S(1)}, f32[4,3,512]{2,1,0:T(4,128)S(1)}, ...), condition=%wide.region_8.9_spmd, body=%wide.region_6.8_spmd.sunk | while | flops 90826240 | bytes 5958033 | solution.py:104
  177.6 3.0 %while.57 = (s32[]{:T(128)}, f32[2,512]{1,0:T(2,128)S(1)}, s32[2,512]{1,0:T(2,128)S(1)}, f32[2,3,512]{2,1,0:T(4,128)S(1)}, bf16[35,2432]{1,0:T(8,128)(2,1)S(1)}, /*index=5*/s32[]{:T(128)}, s32[]{:T(128)}, s32[]{}, s32[]{}) while((s32[]{:T(128)}, f32[2,512]{1,0:T(2,128)S(1)}, s32[2,512]{1,0:T(2,128)S(1)}, f32[2,3,512]{2,1,0:T(4,128)S(1)}, ...), condition=%wide.region_11.12_spmd, body=%wide.region_9.11_spmd.sunk | while | flops 90826240 | bytes 5958033 | solution.py:104
  (257 shorter events, 44.3 us)
Async XLA Ops:
  0.6 16.9 %copy-start = (f32[3,13]{1,0:T(4,128)S(1)}, f32[3,13]{1,0:T(4,128)}, u32[]{:S(2)}) copy-start(f32[3,13]{1,0:T(4,128)} %param.31) | copy-start | bytes 472
  0.6 18.4 %copy-start.3 = (s32[2048]{0:T(1024)S(1)}, s32[2048]{0:T(1024)}, u32[]{:S(2)}) copy-start(s32[2048]{0:T(1024)} %param.24) | copy-start | bytes 24580
  0.7 19.0 %copy-start.4 = (f32[2048]{0:T(1024)S(1)}, f32[2048]{0:T(1024)}, u32[]{:S(2)}) copy-start(f32[2048]{0:T(1024)} %param.22) | copy-start | bytes 24580
  0.7 19.1 %copy-start.2 = (f32[3,2048]{1,0:T(4,128)S(1)}, f32[3,2048]{1,0:T(4,128)}, u32[]{:S(2)}) copy-start(f32[3,2048]{1,0:T(4,128)} %param.23) | copy-start | bytes 73732
  5.9 24.9 %all-to-all-start = ((f32[5,128,8]{2,0,1:T(8,128)}), f32[5,128,8]{2,0,1:T(8,128)}, u32[]{:S(2)}, u32[]{:S(2)}) async-start(f32[5,128,8]{2,0,1:T(8,128)} %copy.17), calls=%async_computation | async-start | bytes 1048576 | tf_op jit(solution)/shard_map/all_to_all | solution.py:169
  19.7 9.6 %copy-start.1 = (f32[3,13]{1,0:T(4,128)S(1)}, f32[3,13]{1,0:T(4,128)}, u32[]{:S(2)}) copy-start(f32[3,13]{1,0:T(4,128)} %param.30) | copy-start | bytes 472
  39.7 7.1 %collective-permute-start = (f32[3,19,128]{2,1,0:T(8,128)S(1)}, f32[3,19,128]{2,1,0:T(8,128)S(1)}, u32[]{:S(2)}, u32[]{:S(2)}) collective-permute-start(f32[3,19,128]{2,1,0:T(8,128)S(1)} %slice.957), channel_id=1, source_target_pairs={{0,8},{8,16},{16,24},{24,32},{32,40},{40,48},{48,56},{56,64},{64,7... | collective-permute-start | bytes 87560 | tf_op jit(solution)/shard_map/ppermute | solution.py:14
  46.8 6.4 %collective-permute-start.1 = (f32[32,3,128]{2,1,0:T(4,128)S(1)}, f32[32,3,128]{2,1,0:T(4,128)S(1)}, u32[]{:S(2)}, u32[]{:S(2)}) collective-permute-start(f32[32,3,128]{2,1,0:T(4,128)S(1)} %slice.1158), channel_id=1, source_target_pairs={{0,1},{1,2},{2,3},{3,4},{4,5},{5,6},{6,7},{7,0},{8,9},{9,10},{10,1... | collective-permute-start | bytes 147464 | tf_op jit(solution)/shard_map/ppermute | solution.py:14
  78.6 5.6 %collective-permute-start.7 = (f32[8,8,64]{2,1,0:T(8,128)S(1)}, f32[8,8,64]{2,1,0:T(8,128)S(1)}, u32[]{:S(2)}, u32[]{:S(2)}) collective-permute-start(f32[8,8,64]{2,1,0:T(8,128)S(1)} %get-tuple-element.704), channel_id=1, source_target_pairs={{8,0},{16,8},{24,16},{32,24},{40,32},{48,40},{56,48},{64,56},{72,6... | collective-permute-start | bytes 49160 | tf_op jit(solution)/shard_map/ppermute | solution.py:25
  78.7 7.0 %collective-permute-start.6 = (f32[8,8,64]{2,1,0:T(8,128)S(1)}, f32[8,8,64]{2,1,0:T(8,128)S(1)}, u32[]{:S(2)}, u32[]{:S(2)}) collective-permute-start(f32[8,8,64]{2,1,0:T(8,128)S(1)} %get-tuple-element.703), channel_id=1, source_target_pairs={{0,8},{8,16},{16,24},{24,32},{32,40},{40,48},{48,56},{56,64},{64,7... | collective-permute-start | bytes 49160 | tf_op jit(solution)/shard_map/ppermute | solution.py:24
  79.2 8.7 %collective-permute-start.3 = (f32[9,16,128]{2,1,0:T(8,128)S(1)}, f32[9,16,128]{2,1,0:T(8,128)S(1)}, u32[]{:S(2)}, u32[]{:S(2)}) collective-permute-start(f32[9,16,128]{2,1,0:T(8,128)S(1)} %get-tuple-element.678), channel_id=1, source_target_pairs={{8,0},{16,8},{24,16},{32,24},{40,32},{48,40},{56,48},{64,56},{72,6... | collective-permute-start | bytes 221192 | tf_op jit(solution)/shard_map/ppermute | solution.py:25
  84.2 7.5 %collective-permute-start.2 = (f32[9,16,128]{2,1,0:T(8,128)S(1)}, f32[9,16,128]{2,1,0:T(8,128)S(1)}, u32[]{:S(2)}, u32[]{:S(2)}) collective-permute-start(f32[9,16,128]{2,1,0:T(8,128)S(1)} %get-tuple-element.677), channel_id=1, source_target_pairs={{0,8},{8,16},{16,24},{24,32},{32,40},{40,48},{48,56},{56,64},{64,7... | collective-permute-start | bytes 221192 | tf_op jit(solution)/shard_map/ppermute | solution.py:24
  85.8 8.1 %collective-permute-start.9 = (f32[32,8,64]{2,1,0:T(8,128)S(1)}, f32[32,8,64]{2,1,0:T(8,128)S(1)}, u32[]{:S(2)}, u32[]{:S(2)}) collective-permute-start(f32[32,8,64]{2,1,0:T(8,128)S(1)} %pad_maximum_fusion.3), channel_id=1, source_target_pairs={{1,0},{2,1},{3,2},{4,3},{5,4},{6,5},{7,6},{0,7},{9,8},{10,9},{11,1... | collective-permute-start | bytes 196616 | tf_op jit(solution)/shard_map/ppermute | solution.py:25
  86.8 8.5 %collective-permute-start.8 = (f32[32,8,64]{2,1,0:T(8,128)S(1)}, f32[32,8,64]{2,1,0:T(8,128)S(1)}, u32[]{:S(2)}, u32[]{:S(2)}) collective-permute-start(f32[32,8,64]{2,1,0:T(8,128)S(1)} %pad_maximum_fusion.3), channel_id=1, source_target_pairs={{0,1},{1,2},{2,3},{3,4},{4,5},{5,6},{6,7},{7,0},{8,9},{9,10},{10,1... | collective-permute-start | bytes 196616 | tf_op jit(solution)/shard_map/ppermute | solution.py:24
  91.8 40.0 %collective-permute-start.5 = (f32[50,9,128]{2,1,0:T(8,128)S(1)}, f32[50,9,128]{2,1,0:T(8,128)S(1)}, u32[]{:S(2)}, u32[]{:S(2)}) collective-permute-start(f32[50,9,128]{2,1,0:T(8,128)S(1)} %get-tuple-element.674), channel_id=1, source_target_pairs={{1,0},{2,1},{3,2},{4,3},{5,4},{6,5},{7,6},{0,7},{9,8},{10,9},{11,1... | collective-permute-start | bytes 691208 | tf_op jit(solution)/shard_map/ppermute | solution.py:25
  92.7 39.1 %collective-permute-start.4 = (f32[50,9,128]{2,1,0:T(8,128)S(1)}, f32[50,9,128]{2,1,0:T(8,128)}, u32[]{:S(2)}, u32[]{:S(2)}) collective-permute-start(f32[50,9,128]{2,1,0:T(8,128)S(1)} %get-tuple-element.673), channel_id=1, source_target_pairs={{0,1},{1,2},{2,3},{3,4},{4,5},{5,6},{6,7},{7,0},{8,9},{9,10},{10,1... | collective-permute-start | bytes 691208 | tf_op jit(solution)/shard_map/ppermute | solution.py:24
where the time goes:
time: 184 us; the launch traced here: 183 us
  other arithmetic  92.7 us (50%)
  local copies, waits for them, and re-layouts  33.2 us (18%)
  starting transfers between devices  21.9 us (12%)
  waiting for transfers between devices  17 us (9%)
  matrix products  14.7 us (8%)
  between operations  1.84 us (1%)
    add x4, other arithmetic, along(): summed + filter_taps[tap_index] * lax.slice_in_dim(field, offset + tap_in...  34 us
    convert_element_type x1, other arithmetic, on_device(): half_grid = field_ext.astype(jnp.bfloat16).reshape(CX + 3, (CY + 3) * NZ)  18.6 us
    reshape x1, local copies, waits for them, and re-layouts, coarsen(): field.reshape(size_a // 2, 2, size_b // 2, 2, size_c // 2, 2)  18.1 us
    add x1, other arithmetic, beside_all(): summed + filter_taps[tap_index] * jnp.roll(field, half_width - tap_index,...  17 us
    all_to_all x1, starting transfers between devices, on_device(): lax.all_to_all(packed.reshape(5, devices, slots), ('gx', 'gy'), split_axi...  11.7 us
    ppermute x2, waiting for transfers between devices, from_behind(): return lax.ppermute(value, axis, pairs)  9.57 us
    dot_general x6, matrix products, advance(): lax.dot_general(x_charge, yz_weights, (((0,), (0,)), ((), ())), preferred...  8.92 us
    convert_element_type x12, other arithmetic, factors(): (y_weights[:, :, None] * z_weights[:, None, :]).astype(jnp.bfloat16)  7.11 us
  transfers between devices with their start and end apart: 11, of which 6 were waited for; matrix products, arithmetic and copies ran while one was open for 28% of the time, Pallas kernels for 0%

commit v1 on v0

v1 whole, which is shorter than its diff:
```python
import functools

import jax
import jax.numpy as jnp
from jax import lax
from jax.experimental import pallas as pl
from jax.experimental.pallas import tpu as pltpu
from jax.sharding import PartitionSpec as P

F32 = jnp.float32
BF16 = jnp.bfloat16
MESH = pl.DeviceIdType.MESH
CX = 32
CY = 16
NZ = 128
TAPS = 13
XP = 40
YR = 19
YP = 20
CP = 24
ROWS = YP * XP
RES = 2048
ARR = 1024
ATOMS = RES + ARR
MOV = 512
FH = 9
CH = 4


def iota(shape, dim):
    return lax.broadcasted_iota(jnp.int32, shape, dim)


def split2(v):
    hi = v.astype(BF16)
    return hi, (v - hi.astype(F32)).astype(BF16)


def split3(v):
    hi = v.astype(BF16)
    rest = v - hi.astype(F32)
    mid = rest.astype(BF16)
    return hi, mid, (rest - mid.astype(F32)).astype(BF16)


def dot_nt(a, b):
    return lax.dot_general(a, b, (((1,), (1,)), ((), ())), preferred_element_type=F32)


def dot_nn(a, b):
    return lax.dot_general(a, b, (((1,), (0,)), ((), ())), preferred_element_type=F32)


def spline(u):
    r = 1.0 - u
    s = u * u
    c = s * u
    return (
        r * r * r * (1.0 / 6.0),
        (3.0 * c - 6.0 * s + 4.0) * (1.0 / 6.0),
        (-3.0 * c + 3.0 * s + 3.0 * u + 1.0) * (1.0 / 6.0),
        c * (1.0 / 6.0),
    )


def pick(d, w, row):
    out = jnp.zeros(d.shape, F32)
    for k in range(4):
        out = jnp.where(d == k, w[k][row : row + 1], out)
    return out


def build_group(lane0, charge, weights, row, cell, a_ref, wx_ref, wy_ref, wz_ref):
    lanes = pl.ds(pl.multiple_of(lane0, 128), 128)
    cx = lax.shift_right_logical(cell, 11)
    cy = lax.shift_right_logical(cell, 7) & 15
    cz = cell & 127
    wx = pick(iota((XP, 128), 0) - cx, weights, row)
    wy = pick(iota((CP, 128), 0) - cy, weights, row + 1)
    wz = pick((iota((NZ, 128), 0) - cz) & 127, weights, row + 2)
    wx_ref[:, lanes] = wx
    wy_ref[:, lanes] = wy
    hi, lo = split2(wz)
    wz_ref[0:NZ, lanes] = hi
    wz_ref[NZ : 2 * NZ, lanes] = lo
    wxq = wx * charge
    for p in range(YP // 2):
        blk = jnp.concatenate(
            [wy[2 * p : 2 * p + 1] * wxq, wy[2 * p + 1 : 2 * p + 2] * wxq], axis=0
        )
        a_ref[p * 2 * XP : (p + 1) * 2 * XP, lanes] = blk.astype(BF16)


def spread_chunk(lane0, size, acc_ref, a_ref, wz_ref):
    lanes = pl.ds(pl.multiple_of(lane0, 256), size)
    acc_ref[...] += dot_nt(a_ref[:, lanes], wz_ref[:, lanes])


def tap_sum(t, taps_ref, dim):
    out = jnp.zeros(t.shape, F32)
    for k in range(TAPS):
        out = jnp.where(t == k, taps_ref[dim, k], out)
    return out


def kernel(
    nx,
    ny,
    rq_ref,
    rf_ref,
    rc_ref,
    count_ref,
    mq_ref,
    mf_ref,
    mc_ref,
    md_ref,
    ft_ref,
    ct_ref,
    res_ref,
    arr_ref,
    grid_ref,
    pay_ref,
    snd_ref,
    b1_ref,
    t2_ref,
    r2_ref,
    rt_ref,
    a_ref,
    wx_ref,
    wy_ref,
    wz_ref,
    acc_ref,
    gf_ref,
    xs_ref,
    xl_ref,
    xr_ref,
    xh_ref,
    bx_ref,
    zf_ref,
    zc_ref,
    f_ref,
    c3_ref,
    fl_ref,
    fr_ref,
    cl_ref,
    cr_ref,
    fin_ref,
    cin_ref,
    fo_ref,
    up_ref,
    hb_ref,
    ao_ref,
    s1_sem,
    r1_sem,
    s2_sem,
    r2_sem,
    sx_sem,
    rx_sem,
    sy_sem,
    ry_sem,
):
    gx = lax.axis_index("gx")
    gy = lax.axis_index("gy")

    barrier = pltpu.get_barrier_semaphore()
    for k in range(1, ny):
        pl.semaphore_signal(
            barrier, inc=1, device_id=(gx, lax.rem(gy + k, ny)), device_id_type=MESH
        )
    for k in range(1, nx):
        pl.semaphore_signal(
            barrier, inc=1, device_id=(lax.rem(gx + k, nx), gy), device_id_type=MESH
        )

    with jax.named_scope("pack"):
        dest = md_ref[...]
        row_of = (dest & (ny - 1)) * nx + lax.div(dest, ny)
        hot = jnp.where(iota((nx * ny, MOV), 0) == row_of, 1.0, 0.0)
        hot16 = hot.astype(BF16)
        earlier = jnp.where(iota((MOV, MOV), 0) < iota((MOV, MOV), 1), 1.0, 0.0)
        counts = dot_nn(hot16, earlier.astype(BF16))
        slot = jnp.sum(hot * counts, axis=0, keepdims=True)
        pay_ref[0:1, :] = mq_ref[...]
        pay_ref[1:4, :] = mf_ref[...]
        pay_ref[4:5, :] = mc_ref[...].astype(F32) + 1.0
        pay_ref[5:8, :] = jnp.zeros((3, MOV), F32)
        pay = pay_ref[...]
        spots = jnp.concatenate([jnp.where(slot == float(s), pay, 0.0) for s in range(8)], axis=0)
        hi, mid, lo = split3(spots)
        packed = dot_nt(hot16, hi) + dot_nt(hot16, mid) + dot_nt(hot16, lo)
        snd_ref[:, 0:64] = packed
        snd_ref[:, 64:128] = jnp.zeros((nx * ny, 64), F32)

    pl.semaphore_wait(barrier, nx + ny - 2)

    def hop1(k):
        to = lax.rem(gy + k, ny)
        return pltpu.make_async_remote_copy(
            src_ref=snd_ref.at[pl.ds(pl.multiple_of(to * nx, nx), nx), :],
            dst_ref=b1_ref.at[pl.ds(pl.multiple_of(gy * nx, nx), nx), :],
            send_sem=s1_sem.at[k],
            recv_sem=r1_sem.at[k],
            device_id=(gx, to),
            device_id_type=MESH,
        )

    for k in range(1, ny):
        hop1(k).start()
    mine = pl.ds(pl.multiple_of(gy * nx, nx), nx)
    b1_ref[mine, :] = snd_ref[mine, :]

    def build_res(g, carry):
        live = iota((1, 128), 1) + g * 128 < count_ref[0]
        charge = jnp.where(live, rq_ref[pl.ds(g, 1), :], 0.0)
        frac = rf_ref[:, pl.ds(pl.multiple_of(g * 128, 128), 128)]
        build_group(
            g * 128, charge, spline(frac), 0, rc_ref[pl.ds(g, 1), :], a_ref, wx_ref, wy_ref, wz_ref
        )
        return carry

    def spread_at(c, carry):
        spread_chunk(c * 512, 512, acc_ref, a_ref, wz_ref)
        return carry

    acc_ref[...] = jnp.zeros_like(acc_ref)
    lax.fori_loop(0, 8, build_res, 0)
    lax.fori_loop(0, 2, spread_at, 0)

    for k in range(1, ny):
        hop1(k).wait()
    for g in range(nx):
        t2_ref[g] = b1_ref[pl.ds(g, ny, stride=nx), :]

    def hop2(k):
        to = lax.rem(gx + k, nx)
        return pltpu.make_async_remote_copy(
            src_ref=t2_ref.at[to],
            dst_ref=r2_ref.at[pl.ds(pl.multiple_of(gx * ny, ny), ny), :],
            send_sem=s2_sem.at[k],
            recv_sem=r2_sem.at[k],
            device_id=(to, gy),
            device_id_type=MESH,
        )

    for k in range(1, nx):
        hop2(k).start()
    r2_ref[pl.ds(pl.multiple_of(gx * ny, ny), ny), :] = t2_ref[gx]

    lax.fori_loop(8, 16, build_res, 0)
    lax.fori_loop(2, 4, spread_at, 0)

    with jax.named_scope("matrices"):
        col = iota((64, 256), 1)
        part = jnp.where(col >= 160, 2, jnp.where(col >= 80, 1, 0))
        base = col - part * 80
        pos = jnp.where(base < 48, base, jnp.where(base < 64, base - 60, base - 32))
        out_x = iota((64, 256), 0)
        fine_t = pos - out_x + 6
        coarse_t = lax.shift_right_arithmetic(pos, 1) - (out_x - XP) + 6
        bx = jnp.where(out_x < XP, tap_sum(fine_t, ft_ref, 0), tap_sum(coarse_t, ct_ref, 0))
        bx_hi = bx.astype(BF16).astype(F32)
        bx = jnp.where(part == 2, bx - bx_hi, bx_hi)
        bx_ref[...] = jnp.where(col < 240, bx, 0.0).astype(BF16)
        t = (iota((NZ, NZ), 0) - iota((NZ, NZ), 1) + 6) & 127
        hi, lo = split2(tap_sum(t, ft_ref, 2))
        zf_ref[0:NZ, 0:NZ] = hi
        zf_ref[NZ : 2 * NZ, 0:NZ] = hi
        zf_ref[0:NZ, NZ : 2 * NZ] = lo
        zf_ref[NZ : 2 * NZ, NZ : 2 * NZ] = jnp.zeros((NZ, NZ), BF16)
        r, c = iota((NZ, 2 * NZ), 0), iota((NZ, 2 * NZ), 1)
        t = ((r & 63) - lax.shift_right_logical(c & 127, 1) + 6) & 63
        zc = tap_sum(t, ct_ref, 2)
        same = lax.shift_right_logical(r, 6) == lax.shift_right_logical(c, 7)
        hi, lo = split2(jnp.where(same, zc, 0.0))
        zc_ref[0:NZ, :] = hi
        zc_ref[NZ : 2 * NZ, :] = hi
        zc_ref[2 * NZ : 3 * NZ, :] = lo

    for k in range(1, nx):
        hop2(k).wait()

    rt_ref[...] = r2_ref[...].T

    def build_arr(s, carry):
        block = rt_ref[pl.ds(pl.multiple_of(s * 8, 8), 8), :]
        cell = jnp.maximum(block[4:5] - 1.0, 0.0).astype(jnp.int32)
        build_group(
            RES + s * 128, block[0:1], spline(block), 1, cell, a_ref, wx_ref, wy_ref, wz_ref
        )
        return carry

    lax.fori_loop(0, 8, build_arr, 0)
    lax.fori_loop(4, 6, spread_at, 0)

    for y in range(YR):
        rows = slice(y * XP, (y + 1) * XP)
        gf_ref[:, y * NZ : (y + 1) * NZ] = acc_ref[rows, 0:NZ] + acc_ref[rows, NZ : 2 * NZ]
    xs_ref[...] = gf_ref[20:36, :]

    up_x = lax.rem(gx + 1, nx)
    down_x = lax.rem(gx + nx - 1, nx)
    up_y = lax.rem(gy + 1, ny)
    down_y = lax.rem(gy + ny - 1, ny)
    x_copies = [
        pltpu.make_async_remote_copy(
            src_ref=xs_ref,
            dst_ref=xl_ref,
            send_sem=sx_sem.at[0],
            recv_sem=rx_sem.at[0],
            device_id=(up_x, gy),
            device_id_type=MESH,
        ),
        pltpu.make_async_remote_copy(
            src_ref=gf_ref.at[pl.ds(0, 16), :],
            dst_ref=xr_ref,
            send_sem=sx_sem.at[1],
            recv_sem=rx_sem.at[1],
            device_id=(down_x, gy),
            device_id_type=MESH,
        ),
    ]
    for copy in x_copies:
        copy.start()
    hi, lo = split2(gf_ref[...])
    zero8 = jnp.zeros((8, YR * NZ), BF16)
    own_hi = jnp.concatenate([hi, zero8], axis=0)
    xh_ref[0:48, :] = own_hi
    xh_ref[160:208, :] = own_hi
    xh_ref[80:128, :] = jnp.concatenate([lo, zero8], axis=0)
    xh_ref[240:256, :] = jnp.zeros((16, YR * NZ), BF16)
    for copy in x_copies:
        copy.wait()
    for at, ref in ((48, xl_ref), (64, xr_ref)):
        hi, lo = split2(ref[...])
        xh_ref[at : at + 16, :] = hi
        xh_ref[at + 160 : at + 176, :] = hi
        xh_ref[at + 80 : at + 96, :] = lo

    conv = dot_nn(bx_ref[...], xh_ref[...])
    f_ref[...] = conv[0:XP]

    r, c = iota((2 * NZ, NZ), 0), iota((2 * NZ, NZ), 1)
    pair = jnp.where(lax.shift_right_logical(r, 1) == c, 1.0, 0.0).astype(BF16)
    coarse = conv[XP : XP + CP]
    tiles = []
    for m in range(5):
        both = []
        for j in (2 * m, 2 * m + 1):
            row = coarse[:, 2 * j * NZ : (2 * j + 1) * NZ]
            if 2 * j + 1 < YR:
                row = row + coarse[:, (2 * j + 1) * NZ : (2 * j + 2) * NZ]
            both.append(row)
        tiles.append(jnp.concatenate(both, axis=1))
    packed = jnp.concatenate(tiles, axis=0)
    hi, lo = split2(packed)
    packed = dot_nn(hi, pair) + dot_nn(lo, pair)
    for m in range(5):
        c3_ref[m] = packed[m * CP : (m + 1) * CP]

    def y_copy(n, src, dst, to):
        return pltpu.make_async_remote_copy(
            src_ref=src,
            dst_ref=dst,
            send_sem=sy_sem.at[n],
            recv_sem=ry_sem.at[n],
            device_id=(gx, to),
            device_id_type=MESH,
        )

    y_copies = [
        y_copy(0, f_ref.at[:, pl.ds(10 * NZ, FH * NZ)], fl_ref, up_y),
        y_copy(1, f_ref.at[:, pl.ds(0, FH * NZ)], fr_ref, down_y),
        y_copy(2, c3_ref.at[pl.ds(1, CH)], cl_ref, up_y),
        y_copy(3, c3_ref.at[pl.ds(0, CH)], cr_ref, down_y),
    ]
    for copy in y_copies:
        copy.start()

    def fine_z(block):
        hi, lo = split2(block)
        both = dot_nn(jnp.concatenate([hi, lo], axis=1), zf_ref[...])
        return both[:, 0:NZ] + both[:, NZ : 2 * NZ]

    def coarse_z(block):
        hi, lo = split2(block)
        return dot_nn(jnp.concatenate([hi, lo], axis=1), zc_ref[0 : 2 * NZ, :]) + dot_nn(
            hi, zc_ref[2 * NZ : 3 * NZ, :]
        )

    def stacked(ref, count):
        return jnp.concatenate([ref[:, y * NZ : (y + 1) * NZ] for y in range(count)], axis=0)

    own = fine_z(stacked(f_ref, YR))
    for y in range(YR):
        fin_ref[:, (y + 6) * NZ : (y + 7) * NZ] = own[y * XP : (y + 1) * XP]
    zero = jnp.zeros((XP, 6 * NZ), F32)
    fin_ref[:, 0 : 6 * NZ] = zero
    fin_ref[:, 25 * NZ : 31 * NZ] = zero
    own = coarse_z(jnp.concatenate([c3_ref[m] for m in range(5)], axis=0))
    zero = jnp.zeros((CP, 6 * NZ), F32)
    cin_ref[:, 0 : 6 * NZ] = zero
    cin_ref[:, 16 * NZ : 22 * NZ] = zero
    for m in range(5):
        cin_ref[:, (2 * m + 6) * NZ : (2 * m + 8) * NZ] = own[m * CP : (m + 1) * CP]

    for copy in y_copies:
        copy.wait()
    for ref, at in ((fl_ref, 0), (fr_ref, 22)):
        halo = fine_z(stacked(ref, FH))
        for y in range(FH):
            fin_ref[:, (y + at) * NZ : (y + at + 1) * NZ] += halo[y * XP : (y + 1) * XP]
    for ref, at in ((cl_ref, 0), (cr_ref, 14)):
        halo = coarse_z(jnp.concatenate([ref[m] for m in range(CH)], axis=0))
        for m in range(CH):
            cin_ref[:, (2 * m + at) * NZ : (2 * m + at + 2) * NZ] += halo[m * CP : (m + 1) * CP]

    def fine_y(i, carry):
        rows = pl.ds(pl.multiple_of(i * 8, 8), 8)
        out = jnp.zeros((8, YR * NZ), F32)
        for k in range(TAPS):
            out = out + ft_ref[1, k] * fin_ref[rows, k * NZ : (k + YR) * NZ]
        fo_ref[rows, 0 : YR * NZ] = out
        fo_ref[rows, YR * NZ : YP * NZ] = jnp.zeros((8, NZ), F32)
        return carry

    lax.fori_loop(0, XP // 8, fine_y, 0)

    def coarse_y(i, carry):
        rows = pl.ds(pl.multiple_of(i * 8, 8), 8)
        out = jnp.zeros((8, 10 * NZ), F32)
        for k in range(TAPS):
            out = out + ct_ref[1, k] * cin_ref[rows, k * NZ : (k + 10) * NZ]
        for j in range(10):
            one = out[:, j * NZ : (j + 1) * NZ]
            up_ref[j, pl.ds(i * 16, 8, stride=2), :] = one
            up_ref[j, pl.ds(i * 16 + 1, 8, stride=2), :] = one
        return carry

    lax.fori_loop(0, CP // 8, coarse_y, 0)

    for p in range(YP // 2):
        add = up_ref[p, 0:XP, :]
        rows = []
        for y in (2 * p, 2 * p + 1):
            total = fo_ref[:, y * NZ : (y + 1) * NZ] + add
            if y < CY:
                for i in range(CX // 8):
                    grid_ref[pl.ds(y + i * 8 * CY, 8, stride=CY), :] = total[i * 8 : i * 8 + 8]
            rows.append(total)
        half = jnp.concatenate(rows, axis=0).astype(BF16)
        hb_ref[p * 2 * XP : (p + 1) * 2 * XP, 0:NZ] = half
        hb_ref[p * 2 * XP : (p + 1) * 2 * XP, NZ : 2 * NZ] = half

    def sample_at(c):
        lanes = pl.ds(pl.multiple_of(c * 256, 256), 256)
        values = dot_nn(hb_ref[...], wz_ref[:, lanes])
        wy = wy_ref[:, lanes]
        part = jnp.zeros((XP, 256), F32)
        for y in range(YR):
            part = part + wy[y : y + 1] * values[y * XP : (y + 1) * XP]
        return jnp.sum(part * wx_ref[:, lanes], axis=0, keepdims=True)

    def sample_res(c, carry):
        value = sample_at(c)
        live = iota((1, 256), 1) + c * 256 < count_ref[0]
        value = jnp.where(live, value, 0.0)
        res_ref[pl.ds(2 * c, 1), :] = value[:, 0:128]
        res_ref[pl.ds(2 * c + 1, 1), :] = value[:, 128:256]
        return carry

    def sample_arr(c, carry):
        value = sample_at(c + RES // 256)
        ao_ref[pl.ds(2 * c, 1), :] = value[:, 0:128]
        ao_ref[pl.ds(2 * c + 1, 1), :] = value[:, 128:256]
        return carry

    lax.fori_loop(0, RES // 256, sample_res, 0)
    lax.fori_loop(0, ARR // 256, sample_arr, 0)

    occupied = jnp.concatenate([rt_ref[s * 8 + 4 : s * 8 + 5, :] for s in range(8)], axis=0)
    value = jnp.where(occupied > 0.5, ao_ref[...], 0.0)
    hi, mid, lo = split3(value)
    wide = (NZ, ARR)
    spread_to = jnp.where(lax.shift_right_logical(iota(wide, 1), 3) == iota(wide, 0), 1.0, 0.0)
    spread_to = spread_to.astype(BF16)
    flat = dot_nn(hi, spread_to) + dot_nn(mid, spread_to) + dot_nn(lo, spread_to)
    keep = (iota((8, ARR), 1) & 7) == iota((8, ARR), 0)
    arr_ref[...] = jnp.sum(jnp.where(keep, flat, 0.0), axis=0, keepdims=True)


def on_device(rq, rf, rc, count, mq, mf, mc, md, ft, ct):
    nx = lax.axis_size("gx")
    ny = lax.axis_size("gy")
    vmem = pl.BlockSpec(memory_space=pltpu.VMEM)
    smem = pl.BlockSpec(memory_space=pltpu.SMEM)
    lanes = YR * NZ
    dma = pltpu.SemaphoreType.DMA
    res, arr, grid = pl.pallas_call(
        functools.partial(kernel, nx, ny),
        out_shape=(
            jax.ShapeDtypeStruct((16, 128), F32),
            jax.ShapeDtypeStruct((1, ARR), F32),
            jax.ShapeDtypeStruct((CX * CY, NZ), F32),
        ),
        in_specs=[vmem, vmem, vmem, smem, vmem, vmem, vmem, vmem, smem, smem],
        out_specs=(vmem, vmem, vmem),
        scratch_shapes=[
            pltpu.VMEM((8, MOV), F32),
            pltpu.VMEM((128, 128), F32),
            pltpu.VMEM((128, 128), F32),
            pltpu.VMEM((nx, ny, 128), F32),
            pltpu.VMEM((128, 128), F32),
            pltpu.VMEM((128, 128), F32),
            pltpu.VMEM((ROWS, ATOMS), BF16),
            pltpu.VMEM((XP, ATOMS), F32),
            pltpu.VMEM((CP, ATOMS), F32),
            pltpu.VMEM((2 * NZ, ATOMS), BF16),
            pltpu.VMEM((ROWS, 2 * NZ), F32),
            pltpu.VMEM((XP, lanes), F32),
            pltpu.VMEM((16, lanes), F32),
            pltpu.VMEM((16, lanes), F32),
            pltpu.VMEM((16, lanes), F32),
            pltpu.VMEM((256, lanes), BF16),
            pltpu.VMEM((64, 256), BF16),
            pltpu.VMEM((2 * NZ, 2 * NZ), BF16),
            pltpu.VMEM((3 * NZ, 2 * NZ), BF16),
            pltpu.VMEM((XP, lanes), F32),
            pltpu.VMEM((5, CP, NZ), F32),
            pltpu.VMEM((XP, FH * NZ), F32),
            pltpu.VMEM((XP, FH * NZ), F32),
            pltpu.VMEM((CH, CP, NZ), F32),
            pltpu.VMEM((CH, CP, NZ), F32),
            pltpu.VMEM((XP, 31 * NZ), F32),
            pltpu.VMEM((CP, 22 * NZ), F32),
            pltpu.VMEM((XP, YP * NZ), F32),
            pltpu.VMEM((10, 2 * CP, NZ), F32),
            pltpu.VMEM((ROWS, 2 * NZ), BF16),
            pltpu.VMEM((8, 128), F32),
            dma((ny,)),
            dma((ny,)),
            dma((nx,)),
            dma((nx,)),
            dma((2,)),
            dma((2,)),
            dma((4,)),
            dma((4,)),
        ],
        compiler_params=pltpu.CompilerParams(
            collective_id=0, has_side_effects=True, vmem_limit_bytes=40 << 20
        ),
        name="multilevel",
    )(
        rq.reshape(16, 128),
        rf,
        rc.reshape(16, 128),
        count,
        mq.reshape(1, MOV),
        mf,
        mc.reshape(1, MOV),
        md.reshape(1, MOV),
        ft,
        ct,
    )
    return res.reshape(RES), arr, grid.reshape(CX, CY, NZ)


def solution(mesh):
    both = ("gx", "gy")
    return jax.shard_map(
        on_device,
        mesh=mesh,
        in_specs=(
            P(both),
            P(None, both),
            P(both),
            P(both),
            P(both),
            P(None, both),
            P(both),
            P(both, None),
            P(),
            P(),
        ),
        out_specs=(P(both), P(both, None), P("gx", "gy", None)),
        check_vma=False,
    )
```

time: 184 us -> 44.9 us (0.24)
  other arithmetic: 92.7 us -> 0 us
  Pallas kernels: 0 us -> 35.7 us
  local copies, waits for them, and re-layouts: 33.2 us -> 7.45 us
  starting transfers between devices: 21.9 us -> 0 us
  waiting for transfers between devices: 17 us -> 0 us
  matrix products: 14.7 us -> 0 us
    add x57 -> x0, other arithmetic: 54.4 us -> none  [the longest x4 34 us: along(): summed + filter_taps[tap_index] * lax.slice_in_dim(field, offset + tap_in...]
    pallas_call x0 -> x1, Pallas kernels: none -> 35.7 us  [on_device(): pl.pallas_call(functools.partial(kernel, nx, ny), out_shape=(jax.ShapeDty...]
    convert_element_type x21 -> x0, other arithmetic: 27.3 us -> none  [the longest x1 18.6 us: on_device(): half_grid = field_ext.astype(jnp.bfloat16).reshape(CX + 3, (CY + 3) * NZ)]
    reshape x8 -> x0, local copies, waits for them, and re-layouts: 19.8 us -> none  [the longest x1 18.1 us: coarsen(): field.reshape(size_a // 2, 2, size_b // 2, 2, size_c // 2, 2)]
    ppermute x10 -> x0, waiting for transfers between devices: 16.4 us -> none  [the longest x2 9.57 us: from_behind(): return lax.ppermute(value, axis, pairs)]
    dot_general x14 -> x0, matrix products: 14.7 us -> none  [the longest x6 8.92 us: advance(): lax.dot_general(x_charge, yz_weights, (((0,), (0,)), ((), ())), preferred...]
    all_to_all x1 -> x0, starting transfers between devices: 11.7 us -> none  [on_device(): lax.all_to_all(packed.reshape(5, devices, slots), ('gx', 'gy'), split_axi...]
    slice x56 -> x0, local copies, waits for them, and re-layouts: 11.2 us -> none  [the longest x6 4.1 us: beside_all(): filter_taps[tap_index] * jnp.roll(field, half_width - tap_index, axis=2)]
  transfers between devices with their start and end apart: 11 -> 0, of which waited for: 6 -> 0; matrix products, arithmetic and copies ran while one was open for 28% -> 0% of each run, Pallas kernels for 0% -> 0%
where the time goes in v1:
time: 44.9 us; the launch traced here: 44.5 us
  Pallas kernels  35.7 us (80%)
  local copies, waits for them, and re-layouts  7.45 us (17%)
  between operations  1.33 us (3%)
    pallas_call x1, Pallas kernels, on_device(): pl.pallas_call(functools.partial(kernel, nx, ny), out_shape=(jax.ShapeDty...  35.7 us
    unnamed x21, local copies, waits for them, and re-layouts  7.45 us

profile of v1, /device:TPU:0, one launch (start us, length us, event | category | flops | bytes accessed | tf_op | source)
XLA Modules:
  0.0 44.5 jit_solution(4931297531173282962)
XLA Ops:
  0.6 0.0 copy-start.1
  1.3 0.0 copy-start.4
  1.3 0.0 copy-done.1
  1.3 0.7 %copy-done.4 = f32[512]{0:T(512)S(1)} copy-done((f32[512]{0:T(512)S(1)}, f32[512]{0:T(512)}, u32[]{:S(2)}) %copy-start.4) | copy-done | bytes 2072
  2.0 0.0 copy-start
  2.0 0.8 %copy-done = f32[3,2048]{1,0:T(4,128)S(1)} copy-done((f32[3,2048]{1,0:T(4,128)S(1)}, f32[3,2048]{1,0:T(4,128)}, u32[]{:S(2)}) %copy-start) | copy-done | bytes 24600
  2.7 0.0 copy-start.2
  2.7 0.7 %copy-done.2 = s32[2048]{0:T(1024)S(1)} copy-done((s32[2048]{0:T(1024)S(1)}, s32[2048]{0:T(1024)}, u32[]{:S(2)}) %copy-start.2) | copy-done | bytes 8216
  3.4 0.0 copy-start.3
  3.4 0.7 %copy-done.3 = f32[3,512]{1,0:T(4,128)S(1)} copy-done((f32[3,512]{1,0:T(4,128)S(1)}, f32[3,512]{1,0:T(4,128)}, u32[]{:S(2)}) %copy-start.3) | copy-done | bytes 6168
  4.1 0.0 copy-start.5
  4.1 0.7 %copy-done.5 = s32[512]{0:T(512)S(1)} copy-done((s32[512]{0:T(512)S(1)}, s32[512]{0:T(512)}, u32[]{:S(2)}) %copy-start.5) | copy-done | bytes 2072
  4.8 0.0 copy-start.6
  4.8 0.7 %copy-done.6 = s32[512,1]{0,1:T(1,128)S(1)} copy-done((s32[512,1]{0,1:T(1,128)S(1)}, s32[512,1]{0,1:T(1,128)}, u32[]{:S(2)}) %copy-start.6) | copy-done | bytes 2072
  5.5 0.0 copy-start.7
  5.5 0.7 %copy-done.7 = f32[3,13]{1,0:T(4,128)S(1)} copy-done((f32[3,13]{1,0:T(4,128)S(1)}, f32[3,13]{1,0:T(4,128)}, u32[]{:S(2)}) %copy-start.7) | copy-done | bytes 180
  6.2 0.0 copy-start.8
  6.2 0.7 %copy-done.8 = f32[3,13]{1,0:T(4,128)S(1)} copy-done((f32[3,13]{1,0:T(4,128)S(1)}, f32[3,13]{1,0:T(4,128)}, u32[]{:S(2)}) %copy-start.8) | copy-done | bytes 180
  6.9 35.7 %multilevel.1 = (f32[16,128]{1,0:T(8,128)S(1)}, f32[1,1024]{1,0:T(1,128)S(1)}, f32[512,128]{1,0:T(8,128)S(1)}) custom-call(f32[16,128]{1,0:T(8,128)S(1)} %bitcast.8, f32[3,2048]{1,0:T(4,128)S(1)} %copy-done, s32[16,128]{1,0:T(8,128)S(1)} %bitcast.9, s32[1]{0:T(128)S(6)} %copy.16.count_ref, f32[1,512]{1,0:T(1,128)S(1)} %bitcast.11, f32[3,512]{1,0:T(4,128)S(1)} %copy-done.3, ...), custom_call_target="tpu_custom_call" | custom-call | tf_op jit(solution)/shard_map/multilevel/pallas_call | solution.py:498
  42.6 0.6 %copy.17 = f32[2048]{0:T(1024)} copy(f32[2048]{0:T(1024)S(1)} %bitcast.10) | data formatting | bytes 16384
  43.2 0.6 %copy.18 = f32[1,1024]{1,0:T(1,128)} copy(f32[1,1024]{1,0:T(1,128)S(1)} %get-tuple-element.13) | data formatting | bytes 8192
  43.8 0.7 %copy.19 = f32[32,16,128]{2,1,0:T(8,128)} copy(f32[32,16,128]{2,1,0:T(8,128)S(1)} %bitcast.7) | data formatting | bytes 524288
Async XLA Ops:
  0.6 0.7 %copy-start.1 = (f32[2048]{0:T(1024)S(1)}, f32[2048]{0:T(1024)}, u32[]{:S(2)}) copy-start(f32[2048]{0:T(1024)} %param.10) | copy-start | bytes 24580
  1.3 0.7 %copy-start.4 = (f32[512]{0:T(512)S(1)}, f32[512]{0:T(512)}, u32[]{:S(2)}) copy-start(f32[512]{0:T(512)} %param.14) | copy-start | bytes 6148
  2.0 0.8 %copy-start = (f32[3,2048]{1,0:T(4,128)S(1)}, f32[3,2048]{1,0:T(4,128)}, u32[]{:S(2)}) copy-start(f32[3,2048]{1,0:T(4,128)} %rf_ref.1) | copy-start | bytes 73732
  2.7 0.7 %copy-start.2 = (s32[2048]{0:T(1024)S(1)}, s32[2048]{0:T(1024)}, u32[]{:S(2)}) copy-start(s32[2048]{0:T(1024)} %param.12) | copy-start | bytes 24580
  3.4 0.7 %copy-start.3 = (f32[3,512]{1,0:T(4,128)S(1)}, f32[3,512]{1,0:T(4,128)}, u32[]{:S(2)}) copy-start(f32[3,512]{1,0:T(4,128)} %mf_ref.1) | copy-start | bytes 18436
  4.1 0.7 %copy-start.5 = (s32[512]{0:T(512)S(1)}, s32[512]{0:T(512)}, u32[]{:S(2)}) copy-start(s32[512]{0:T(512)} %param.16) | copy-start | bytes 6148
  4.8 0.7 %copy-start.6 = (s32[512,1]{0,1:T(1,128)S(1)}, s32[512,1]{0,1:T(1,128)}, u32[]{:S(2)}) copy-start(s32[512,1]{0,1:T(1,128)} %param.17) | copy-start | bytes 6148
  5.5 0.7 %copy-start.7 = (f32[3,13]{1,0:T(4,128)S(1)}, f32[3,13]{1,0:T(4,128)}, u32[]{:S(2)}) copy-start(f32[3,13]{1,0:T(4,128)} %ft_ref.1) | copy-start | bytes 472
  6.2 0.7 %copy-start.8 = (f32[3,13]{1,0:T(4,128)S(1)}, f32[3,13]{1,0:T(4,128)}, u32[]{:S(2)}) copy-start(f32[3,13]{1,0:T(4,128)} %ct_ref.1) | copy-start | bytes 472

commit v2 on v1

--- a/solution.py
+++ b/solution.py
@@ -70,25 +70,29 @@
     return out
 
 
-def build_group(lane0, charge, weights, row, cell, a_ref, wx_ref, wy_ref, wz_ref):
+def build_group(block, lane0, x0, a_ref, wz_ref, own):
     lanes = pl.ds(pl.multiple_of(lane0, 128), 128)
-    cx = lax.shift_right_logical(cell, 11)
+    xrows = XP if own is not None else 16
+    weights = spline(block)
+    cell = jnp.maximum(block[4:5] - 1.0, 0.0).astype(jnp.int32)
+    cx = lax.shift_right_logical(cell, 11) - x0
     cy = lax.shift_right_logical(cell, 7) & 15
     cz = cell & 127
-    wx = pick(iota((XP, 128), 0) - cx, weights, row)
-    wy = pick(iota((CP, 128), 0) - cy, weights, row + 1)
-    wz = pick((iota((NZ, 128), 0) - cz) & 127, weights, row + 2)
-    wx_ref[:, lanes] = wx
-    wy_ref[:, lanes] = wy
+    wx = pick(iota((xrows, 128), 0) - cx, weights, 1)
+    wy = pick(iota((CP, 128), 0) - cy, weights, 2)
+    wz = pick((iota((NZ, 128), 0) - cz) & 127, weights, 3)
+    if own is not None:
+        own[0][:, lanes] = wx
+        own[1][:, lanes] = wy
     hi, lo = split2(wz)
     wz_ref[0:NZ, lanes] = hi
     wz_ref[NZ : 2 * NZ, lanes] = lo
-    wxq = wx * charge
+    wxq = wx * block[0:1]
     for p in range(YP // 2):
         blk = jnp.concatenate(
             [wy[2 * p : 2 * p + 1] * wxq, wy[2 * p + 1 : 2 * p + 2] * wxq], axis=0
         )
-        a_ref[p * 2 * XP : (p + 1) * 2 * XP, lanes] = blk.astype(BF16)
+        a_ref[p * 2 * xrows : (p + 1) * 2 * xrows, lanes] = blk.astype(BF16)
 
 
 def spread_chunk(lane0, size, acc_ref, a_ref, wz_ref):
@@ -106,6 +110,22 @@
 def kernel(
     nx,
     ny,
+    rq_hbm,
+    rf_hbm,
+    rc_hbm,
+    count_hbm,
+    mq_hbm,
+    mf_hbm,
+    mc_hbm,
+    md_hbm,
+    ft_hbm,
+    ct_hbm,
+    res_hbm,
+    arr_hbm,
+    grid_hbm,
+    res_ref,
+    arr_ref,
+    grid_ref,
     rq_ref,
     rf_ref,
     rc_ref,
@@ -116,24 +136,26 @@
     md_ref,
     ft_ref,
     ct_ref,
-    res_ref,
-    arr_ref,
-    grid_ref,
     pay_ref,
     snd_ref,
     b1_ref,
     t2_ref,
     r2_ref,
     rt_ref,
+    rb_ref,
+    rl_ref,
+    rr_ref,
     a_ref,
+    al_ref,
+    ar_ref,
     wx_ref,
     wy_ref,
     wz_ref,
+    wl_ref,
+    wr_ref,
     acc_ref,
-    gf_ref,
-    xs_ref,
-    xl_ref,
-    xr_ref,
+    accl_ref,
+    accr_ref,
     xh_ref,
     bx_ref,
     zf_ref,
@@ -150,6 +172,8 @@
     up_ref,
     hb_ref,
     ao_ref,
+    in_sem,
+    out_sem,
     s1_sem,
     r1_sem,
     s2_sem,
@@ -162,6 +186,26 @@
     gx = lax.axis_index("gx")
     gy = lax.axis_index("gy")
 
+    inputs = [
+        pltpu.make_async_copy(src, dst, in_sem.at[n])
+        for n, (src, dst) in enumerate(
+            (
+                (md_hbm, md_ref),
+                (mq_hbm, mq_ref),
+                (mf_hbm, mf_ref),
+                (mc_hbm, mc_ref),
+                (count_hbm, count_ref),
+                (rq_hbm, rq_ref),
+                (rf_hbm, rf_ref),
+                (rc_hbm, rc_ref),
+                (ft_hbm, ft_ref),
+                (ct_hbm, ct_ref),
+            )
+        )
+    ]
+    for copy in inputs:
+        copy.start()
+
     barrier = pltpu.get_barrier_semaphore()
     for k in range(1, ny):
         pl.semaphore_signal(
@@ -171,6 +215,8 @@
         pl.semaphore_signal(
             barrier, inc=1, device_id=(lax.rem(gx + k, nx), gy), device_id_type=MESH
         )
+    for copy in inputs[:4]:
+        copy.wait()
 
     with jax.named_scope("pack"):
         dest = md_ref[...]
@@ -209,33 +255,57 @@
     mine = pl.ds(pl.multiple_of(gy * nx, nx), nx)
     b1_ref[mine, :] = snd_ref[mine, :]
 
-    def build_res(g, carry):
+    for copy in inputs[4:]:
+        copy.wait()
+    for g in range(RES // 128):
         live = iota((1, 128), 1) + g * 128 < count_ref[0]
-        charge = jnp.where(live, rq_ref[pl.ds(g, 1), :], 0.0)
-        frac = rf_ref[:, pl.ds(pl.multiple_of(g * 128, 128), 128)]
-        build_group(
-            g * 128, charge, spline(frac), 0, rc_ref[pl.ds(g, 1), :], a_ref, wx_ref, wy_ref, wz_ref
-        )
-        return carry
-
-    def spread_at(c, carry):
+        rb_ref[g, 0:1, :] = jnp.where(live, rq_ref[g : g + 1, :], 0.0)
+        rb_ref[g, 1:4, :] = rf_ref[:, g * 128 : (g + 1) * 128]
+        rb_ref[g, 4:5, :] = rc_ref[g : g + 1, :].astype(F32) + 1.0
+        rb_ref[g, 5:8, :] = jnp.zeros((3, 128), F32)
+
+    def x_copy(n, dst, to):
+        return pltpu.make_async_remote_copy(
+            src_ref=rb_ref,
+            dst_ref=dst,
+            send_sem=sx_sem.at[n],
+            recv_sem=rx_sem.at[n],
+            device_id=(to, gy),
+            device_id_type=MESH,
+        )
+
+    x_copies = [
+        x_copy(0, rl_ref, lax.rem(gx + 1, nx)),
+        x_copy(1, rr_ref, lax.rem(gx + nx - 1, nx)),
+    ]
+    for copy in x_copies:
+        copy.start()
+
+    acc_ref[...] = jnp.zeros_like(acc_ref)
+    accl_ref[...] = jnp.zeros_like(accl_ref)
+    accr_ref[...] = jnp.zeros_like(accr_ref)
+
+    def own_res(c, carry):
+        for n in range(4):
+            g = c * 4 + n
+            build_group(rb_ref[g], g * 128, 0, a_ref, wz_ref, (wx_ref, wy_ref))
         spread_chunk(c * 512, 512, acc_ref, a_ref, wz_ref)
         return carry
 
-    acc_ref[...] = jnp.zeros_like(acc_ref)
-    lax.fori_loop(0, 8, build_res, 0)
-    lax.fori_loop(0, 2, spread_at, 0)
+    lax.fori_loop(0, RES // 512, own_res, 0)
 
     for k in range(1, ny):
         hop1(k).wait()
     for g in range(nx):
-        t2_ref[g] = b1_ref[pl.ds(g, ny, stride=nx), :]
+        t2_ref[g + 1] = b1_ref[pl.ds(g, ny, stride=nx), :]
+    t2_ref[0] = t2_ref[nx]
+    t2_ref[nx + 1] = t2_ref[1]
 
     def hop2(k):
         to = lax.rem(gx + k, nx)
         return pltpu.make_async_remote_copy(
-            src_ref=t2_ref.at[to],
-            dst_ref=r2_ref.at[pl.ds(pl.multiple_of(gx * ny, ny), ny), :],
+            src_ref=t2_ref.at[pl.ds(to, 3)],
+            dst_ref=r2_ref.at[gx],
             send_sem=s2_sem.at[k],
             recv_sem=r2_sem.at[k],
             device_id=(to, gy),
@@ -244,10 +314,21 @@
 
     for k in range(1, nx):
         hop2(k).start()
-    r2_ref[pl.ds(pl.multiple_of(gx * ny, ny), ny), :] = t2_ref[gx]
-
-    lax.fori_loop(8, 16, build_res, 0)
-    lax.fori_loop(2, 4, spread_at, 0)
+    r2_ref[gx] = t2_ref[pl.ds(gx, 3)]
+
+    for copy in x_copies:
+        copy.wait()
+
+    def near_res(c, carry):
+        for n in range(4):
+            g = c * 4 + n
+            build_group(rl_ref[g], g * 128, 20, al_ref, wl_ref, None)
+            build_group(rr_ref[g], g * 128, 0, ar_ref, wr_ref, None)
+        spread_chunk(c * 512, 512, accl_ref, al_ref, wl_ref)
+        spread_chunk(c * 512, 512, accr_ref, ar_ref, wr_ref)
+        return carry
+
+    lax.fori_loop(0, RES // 512, near_res, 0)
 
     with jax.named_scope("matrices"):
         col = iota((64, 256), 1)
@@ -279,62 +360,39 @@
     for k in range(1, nx):
         hop2(k).wait()
 
-    rt_ref[...] = r2_ref[...].T
-
-    def build_arr(s, carry):
-        block = rt_ref[pl.ds(pl.multiple_of(s * 8, 8), 8), :]
-        cell = jnp.maximum(block[4:5] - 1.0, 0.0).astype(jnp.int32)
-        build_group(
-            RES + s * 128, block[0:1], spline(block), 1, cell, a_ref, wx_ref, wy_ref, wz_ref
-        )
+    for n in range(3):
+        rt_ref[n] = r2_ref[:, n].reshape(nx * ny, 128).T
+
+    def all_arr(c, carry):
+        for n in range(4):
+            s = c * 4 + n
+            at = RES + s * 128
+            rows = pl.ds(pl.multiple_of(s * 8, 8), 8)
+            build_group(rt_ref[1, rows, :], at, 0, a_ref, wz_ref, (wx_ref, wy_ref))
+            build_group(rt_ref[0, rows, :], at, 20, al_ref, wl_ref, None)
+            build_group(rt_ref[2, rows, :], at, 0, ar_ref, wr_ref, None)
+        spread_chunk(RES + c * 512, 512, acc_ref, a_ref, wz_ref)
+        spread_chunk(RES + c * 512, 512, accl_ref, al_ref, wl_ref)
+        spread_chunk(RES + c * 512, 512, accr_ref, ar_ref, wr_ref)
         return carry
 
-    lax.fori_loop(0, 8, build_arr, 0)
-    lax.fori_loop(4, 6, spread_at, 0)
-
-    for y in range(YR):
-        rows = slice(y * XP, (y + 1) * XP)
-        gf_ref[:, y * NZ : (y + 1) * NZ] = acc_ref[rows, 0:NZ] + acc_ref[rows, NZ : 2 * NZ]
-    xs_ref[...] = gf_ref[20:36, :]
-
-    up_x = lax.rem(gx + 1, nx)
-    down_x = lax.rem(gx + nx - 1, nx)
+    lax.fori_loop(0, ARR // 512, all_arr, 0)
+
     up_y = lax.rem(gy + 1, ny)
     down_y = lax.rem(gy + ny - 1, ny)
-    x_copies = [
-        pltpu.make_async_remote_copy(
-            src_ref=xs_ref,
-            dst_ref=xl_ref,
-            send_sem=sx_sem.at[0],
-            recv_sem=rx_sem.at[0],
-            device_id=(up_x, gy),
-            device_id_type=MESH,
-        ),
-        pltpu.make_async_remote_copy(
-            src_ref=gf_ref.at[pl.ds(0, 16), :],
-            dst_ref=xr_ref,
-            send_sem=sx_sem.at[1],
-            recv_sem=rx_sem.at[1],
-            device_id=(down_x, gy),
-            device_id_type=MESH,
-        ),
-    ]
-    for copy in x_copies:
-        copy.start()
-    hi, lo = split2(gf_ref[...])
-    zero8 = jnp.zeros((8, YR * NZ), BF16)
-    own_hi = jnp.concatenate([hi, zero8], axis=0)
-    xh_ref[0:48, :] = own_hi
-    xh_ref[160:208, :] = own_hi
-    xh_ref[80:128, :] = jnp.concatenate([lo, zero8], axis=0)
-    xh_ref[240:256, :] = jnp.zeros((16, YR * NZ), BF16)
-    for copy in x_copies:
-        copy.wait()
-    for at, ref in ((48, xl_ref), (64, xr_ref)):
-        hi, lo = split2(ref[...])
-        xh_ref[at : at + 16, :] = hi
-        xh_ref[at + 160 : at + 176, :] = hi
-        xh_ref[at + 80 : at + 96, :] = lo
+    for y in range(YR):
+        lanes = slice(y * NZ, (y + 1) * NZ)
+        rows = []
+        for ref, count in ((acc_ref, XP), (accl_ref, 16), (accr_ref, 16)):
+            part = ref[y * count : (y + 1) * count]
+            rows.append(part[:, 0:NZ] + part[:, NZ : 2 * NZ])
+            if count == XP:
+                rows.append(jnp.zeros((8, NZ), F32))
+        hi, lo = split2(jnp.concatenate(rows, axis=0))
+        xh_ref[0:80, lanes] = hi
+        xh_ref[80:160, lanes] = lo
+        xh_ref[160:240, lanes] = hi
+        xh_ref[240:256, lanes] = jnp.zeros((16, NZ), BF16)
 
     conv = dot_nn(bx_ref[...], xh_ref[...])
     f_ref[...] = conv[0:XP]
@@ -451,6 +509,13 @@
         hb_ref[p * 2 * XP : (p + 1) * 2 * XP, 0:NZ] = half
         hb_ref[p * 2 * XP : (p + 1) * 2 * XP, NZ : 2 * NZ] = half
 
+    outputs = [
+        pltpu.make_async_copy(grid_ref, grid_hbm, out_sem.at[0]),
+        pltpu.make_async_copy(res_ref, res_hbm, out_sem.at[1]),
+        pltpu.make_async_copy(arr_ref, arr_hbm, out_sem.at[2]),
+    ]
+    outputs[0].start()
+
     def sample_at(c):
         lanes = pl.ds(pl.multiple_of(c * 256, 256), 256)
         values = dot_nn(hb_ref[...], wz_ref[:, lanes])
@@ -475,9 +540,10 @@
         return carry
 
     lax.fori_loop(0, RES // 256, sample_res, 0)
+    outputs[1].start()
     lax.fori_loop(0, ARR // 256, sample_arr, 0)
 
-    occupied = jnp.concatenate([rt_ref[s * 8 + 4 : s * 8 + 5, :] for s in range(8)], axis=0)
+    occupied = jnp.concatenate([rt_ref[1, s * 8 + 4 : s * 8 + 5, :] for s in range(8)], axis=0)
     value = jnp.where(occupied > 0.5, ao_ref[...], 0.0)
     hi, mid, lo = split3(value)
     wide = (NZ, ARR)
@@ -486,14 +552,30 @@
     flat = dot_nn(hi, spread_to) + dot_nn(mid, spread_to) + dot_nn(lo, spread_to)
     keep = (iota((8, ARR), 1) & 7) == iota((8, ARR), 0)
     arr_ref[...] = jnp.sum(jnp.where(keep, flat, 0.0), axis=0, keepdims=True)
+    outputs[2].start()
+    for copy in outputs:
+        copy.wait()
+
+
+def hand_out(*refs):
+    given, out, held, sems = refs[0:3], refs[3:6], refs[6:9], refs[9]
+    reads = [pltpu.make_async_copy(given[n], held[n], sems.at[n]) for n in range(3)]
+    writes = [pltpu.make_async_copy(held[n], out[n], sems.at[n + 3]) for n in range(3)]
+    for copy in reads:
+        copy.start()
+    for read, write in zip(reads, writes):
+        read.wait()
+        write.start()
+    for copy in writes:
+        copy.wait()
 
 
 def on_device(rq, rf, rc, count, mq, mf, mc, md, ft, ct):
     nx = lax.axis_size("gx")
     ny = lax.axis_size("gy")
-    vmem = pl.BlockSpec(memory_space=pltpu.VMEM)
-    smem = pl.BlockSpec(memory_space=pltpu.SMEM)
+    hbm = pl.BlockSpec(memory_space=pltpu.HBM)
     lanes = YR * NZ
+    near = YP * 16
     dma = pltpu.SemaphoreType.DMA
     res, arr, grid = pl.pallas_call(
         functools.partial(kernel, nx, ny),
@@ -502,24 +584,42 @@
             jax.ShapeDtypeStruct((1, ARR), F32),
             jax.ShapeDtypeStruct((CX * CY, NZ), F32),
         ),
-        in_specs=[vmem, vmem, vmem, smem, vmem, vmem, vmem, vmem, smem, smem],
-        out_specs=(vmem, vmem, vmem),
+        in_specs=[hbm] * 10,
+        out_specs=(hbm, hbm, hbm),
         scratch_shapes=[
+            pltpu.VMEM((16, 128), F32),
+            pltpu.VMEM((1, ARR), F32),
+            pltpu.VMEM((CX * CY, NZ), F32),
+            pltpu.VMEM((16, 128), F32),
+            pltpu.VMEM((3, RES), F32),
+            pltpu.VMEM((16, 128), jnp.int32),
+            pltpu.SMEM((1,), jnp.int32),
+            pltpu.VMEM((1, MOV), F32),
+            pltpu.VMEM((3, MOV), F32),
+            pltpu.VMEM((1, MOV), jnp.int32),
+            pltpu.VMEM((1, MOV), jnp.int32),
+            pltpu.SMEM((3, TAPS), F32),
+            pltpu.SMEM((3, TAPS), F32),
             pltpu.VMEM((8, MOV), F32),
             pltpu.VMEM((128, 128), F32),
             pltpu.VMEM((128, 128), F32),
-            pltpu.VMEM((nx, ny, 128), F32),
-            pltpu.VMEM((128, 128), F32),
-            pltpu.VMEM((128, 128), F32),
+            pltpu.VMEM((nx + 2, ny, 128), F32),
+            pltpu.VMEM((nx, 3, ny, 128), F32),
+            pltpu.VMEM((3, 128, 128), F32),
+            pltpu.VMEM((16, 8, 128), F32),
+            pltpu.VMEM((16, 8, 128), F32),
+            pltpu.VMEM((16, 8, 128), F32),
             pltpu.VMEM((ROWS, ATOMS), BF16),
+            pltpu.VMEM((near, ATOMS), BF16),
+            pltpu.VMEM((near, ATOMS), BF16),
             pltpu.VMEM((XP, ATOMS), F32),
             pltpu.VMEM((CP, ATOMS), F32),
             pltpu.VMEM((2 * NZ, ATOMS), BF16),
+            pltpu.VMEM((2 * NZ, ATOMS), BF16),
+            pltpu.VMEM((2 * NZ, ATOMS), BF16),
             pltpu.VMEM((ROWS, 2 * NZ), F32),
-            pltpu.VMEM((XP, lanes), F32),
-            pltpu.VMEM((16, lanes), F32),
-            pltpu.VMEM((16, lanes), F32),
-            pltpu.VMEM((16, lanes), F32),
+            pltpu.VMEM((near, 2 * NZ), F32),
+            pltpu.VMEM((near, 2 * NZ), F32),
             pltpu.VMEM((256, lanes), BF16),
             pltpu.VMEM((64, 256), BF16),
             pltpu.VMEM((2 * NZ, 2 * NZ), BF16),
@@ -536,6 +636,8 @@
             pltpu.VMEM((10, 2 * CP, NZ), F32),
             pltpu.VMEM((ROWS, 2 * NZ), BF16),
             pltpu.VMEM((8, 128), F32),
+            dma((10,)),
+            dma((3,)),
             dma((ny,)),
             dma((ny,)),
             dma((nx,)),
@@ -546,7 +648,7 @@
             dma((4,)),
         ],
         compiler_params=pltpu.CompilerParams(
-            collective_id=0, has_side_effects=True, vmem_limit_bytes=40 << 20
+            collective_id=0, has_side_effects=True, vmem_limit_bytes=64 << 20
         ),
         name="multilevel",
     )(
@@ -561,6 +663,23 @@
         ft,
         ct,
     )
+    res, arr, grid = pl.pallas_call(
+        hand_out,
+        out_shape=(
+            jax.ShapeDtypeStruct((16, 128), F32),
+            jax.ShapeDtypeStruct((1, ARR), F32),
+            jax.ShapeDtypeStruct((CX * CY, NZ), F32),
+        ),
+        in_specs=[hbm] * 3,
+        out_specs=(hbm, hbm, hbm),
+        scratch_shapes=[
+            pltpu.VMEM((16, 128), F32),
+            pltpu.VMEM((1, ARR), F32),
+            pltpu.VMEM((CX * CY, NZ), F32),
+            dma((6,)),
+        ],
+        name="hand_out",
+    )(res, arr, grid)
     return res.reshape(RES), arr, grid.reshape(CX, CY, NZ)
 
 

time: 44.9 us -> 38.4 us (0.86)
  local copies, waits for them, and re-layouts: 7.45 us -> 0 us
  Pallas kernels: 35.7 us -> 36.4 us
    unnamed x21 -> x0, local copies, waits for them, and re-layouts: 7.45 us -> none
    pallas_call x0 -> x1, Pallas kernels: none -> 1.73 us  [on_device(): pl.pallas_call(hand_out, out_shape=(jax.ShapeDtypeStruct((16, 128), F32),...]
    pallas_call x1, Pallas kernels: 35.7 us -> 34.7 us  [on_device(): pl.pallas_call(functools.partial(kernel, nx, ny), out_shape=(jax.ShapeDty...]
where the time goes in v2:
time: 38.4 us; the launch traced here: 37.7 us
  Pallas kernels  36.4 us (95%)
  between operations  1.29 us (3%)
    pallas_call x1, Pallas kernels, on_device(): pl.pallas_call(functools.partial(kernel, nx, ny), out_shape=(jax.ShapeDty...  34.7 us
    pallas_call x1, Pallas kernels, on_device(): pl.pallas_call(hand_out, out_shape=(jax.ShapeDtypeStruct((16, 128), F32),...  1.73 us

profile of v2, /device:TPU:0, one launch (start us, length us, event | category | flops | bytes accessed | tf_op | source)
XLA Modules:
  0.0 37.7 jit_solution(1028620390814762962)
XLA Ops:
  1.3 34.7 %multilevel.1 = (f32[16,128]{1,0:T(8,128)}, f32[1,1024]{1,0:T(1,128)}, f32[512,128]{1,0:T(8,128)}) custom-call(f32[16,128]{1,0:T(8,128)} %bitcast.7, f32[3,2048]{1,0:T(4,128)} %rf_hbm.1, s32[16,128]{1,0:T(8,128)} %bitcast.8, s32[1]{0:T(128)S(6)} %copy.13.count_hbm, f32[1,512]{1,0:T(1,128)} %bitcast.9, f32[3,512]{1,0:T(4,128)} %mf_hbm.1, s32[1,512]{1,0:T(1,128)} %bitcast.10, ...), custom_call_target="tpu_custom_call" | custom-call | tf_op jit(solution)/shard_map/multilevel/pallas_call | solution.py:580
  36.0 1.7 %hand_out.1 = (f32[16,128]{1,0:T(8,128)}, f32[1,1024]{1,0:T(1,128)}, f32[512,128]{1,0:T(8,128)}) custom-call(f32[16,128]{1,0:T(8,128)} %get-tuple-element.9.refs_0_, f32[1,1024]{1,0:T(1,128)} %get-tuple-element.10.refs_1_, f32[512,128]{1,0:T(8,128)} %get-tuple-element.11.refs_2_), custom_call_target="tpu_custom_call" | custom-call | tf_op jit(solution)/shard_map/hand_out/pallas_call | solution.py:666

commit v3 on v2

--- a/solution.py
+++ b/solution.py
@@ -63,31 +63,44 @@
     )
 
 
-def pick(d, w, row):
-    out = jnp.zeros(d.shape, F32)
+def pick(rows, at, values):
+    out = jnp.zeros(rows.shape, rows.dtype)
     for k in range(4):
-        out = jnp.where(d == k, w[k][row : row + 1], out)
+        out = jnp.where(rows == at[k], values[k], out)
     return out
 
 
-def build_group(block, lane0, x0, a_ref, wz_ref, own):
-    lanes = pl.ds(pl.multiple_of(lane0, 128), 128)
-    xrows = XP if own is not None else 16
-    weights = spline(block)
-    cell = jnp.maximum(block[4:5] - 1.0, 0.0).astype(jnp.int32)
+def prepare(charge, fracs, cells, x0):
+    cell = jnp.maximum(cells - 1.0, 0.0).astype(jnp.int32)
     cx = lax.shift_right_logical(cell, 11) - x0
     cy = lax.shift_right_logical(cell, 7) & 15
     cz = cell & 127
-    wx = pick(iota((xrows, 128), 0) - cx, weights, 1)
-    wy = pick(iota((CP, 128), 0) - cy, weights, 2)
-    wz = pick((iota((NZ, 128), 0) - cz) & 127, weights, 3)
+    steps = range(4)
+    at_x = [cx + k for k in steps]
+    at_y = [cy + k for k in steps]
+    at_z = [((cz + k) & 127).astype(F32) for k in steps]
+    w_x, w_y, w_z = (spline(frac) for frac in fracs)
+    hi = [w.astype(BF16).astype(F32) for w in w_z]
+    lo = [w - h for w, h in zip(w_z, hi)]
+    return charge, at_x, w_x, at_y, w_y, at_z, hi, lo
+
+
+def build_group(rows, s, lane0, a_ref, wz_ref, own):
+    charge, *lists = rows
+    charge = charge[s : s + 1]
+    at_x, w_x, at_y, w_y, at_z, hi, lo = ([v[s : s + 1] for v in each] for each in lists)
+    lanes = lane_window(lane0, 128)
+    xrows = XP if own is not None else 16
+    wx = pick(iota((xrows, 128), 0), at_x, w_x)
+    wy = pick(iota((CP, 128), 0), at_y, w_y)
     if own is not None:
         own[0][:, lanes] = wx
         own[1][:, lanes] = wy
-    hi, lo = split2(wz)
-    wz_ref[0:NZ, lanes] = hi
-    wz_ref[NZ : 2 * NZ, lanes] = lo
-    wxq = wx * block[0:1]
+    z = iota((NZ, 128), 0).astype(BF16)
+    at_z, hi, lo = ([v.astype(BF16) for v in each] for each in (at_z, hi, lo))
+    wz_ref[0:NZ, lanes] = pick(z, at_z, hi)
+    wz_ref[NZ : 2 * NZ, lanes] = pick(z, at_z, lo)
+    wxq = wx * charge
     for p in range(YP // 2):
         blk = jnp.concatenate(
             [wy[2 * p : 2 * p + 1] * wxq, wy[2 * p + 1 : 2 * p + 2] * wxq], axis=0
@@ -95,8 +108,14 @@
         a_ref[p * 2 * xrows : (p + 1) * 2 * xrows, lanes] = blk.astype(BF16)
 
 
+def lane_window(start, size):
+    if isinstance(start, int):
+        return slice(start, start + size)
+    return pl.ds(pl.multiple_of(start, 128), size)
+
+
 def spread_chunk(lane0, size, acc_ref, a_ref, wz_ref):
-    lanes = pl.ds(pl.multiple_of(lane0, 256), size)
+    lanes = lane_window(lane0, size)
     acc_ref[...] += dot_nt(a_ref[:, lanes], wz_ref[:, lanes])
 
 
@@ -229,9 +248,12 @@
         pay_ref[0:1, :] = mq_ref[...]
         pay_ref[1:4, :] = mf_ref[...]
         pay_ref[4:5, :] = mc_ref[...].astype(F32) + 1.0
-        pay_ref[5:8, :] = jnp.zeros((3, MOV), F32)
-        pay = pay_ref[...]
-        spots = jnp.concatenate([jnp.where(slot == float(s), pay, 0.0) for s in range(8)], axis=0)
+        at_slot = iota((8, MOV), 0).astype(F32) == slot
+        spots = jnp.concatenate(
+            [jnp.where(at_slot, pay_ref[n : n + 1, :], 0.0) for n in range(5)]
+            + [jnp.zeros((24, MOV), F32)],
+            axis=0,
+        )
         hi, mid, lo = split3(spots)
         packed = dot_nt(hot16, hi) + dot_nt(hot16, mid) + dot_nt(hot16, lo)
         snd_ref[:, 0:64] = packed
@@ -257,12 +279,11 @@
 
     for copy in inputs[4:]:
         copy.wait()
-    for g in range(RES // 128):
-        live = iota((1, 128), 1) + g * 128 < count_ref[0]
-        rb_ref[g, 0:1, :] = jnp.where(live, rq_ref[g : g + 1, :], 0.0)
-        rb_ref[g, 1:4, :] = rf_ref[:, g * 128 : (g + 1) * 128]
-        rb_ref[g, 4:5, :] = rc_ref[g : g + 1, :].astype(F32) + 1.0
-        rb_ref[g, 5:8, :] = jnp.zeros((3, 128), F32)
+    rb_ref[0] = jnp.where(iota((16, 128), 0) * 128 < count_ref[0], rq_ref[...], 0.0)
+    for d in range(3):
+        for g in range(RES // 128):
+            rb_ref[1 + d, g : g + 1, :] = rf_ref[d : d + 1, g * 128 : (g + 1) * 128]
+    rb_ref[4] = rc_ref[...].astype(F32) + 1.0
 
     def x_copy(n, dst, to):
         return pltpu.make_async_remote_copy(
@@ -285,14 +306,17 @@
     accl_ref[...] = jnp.zeros_like(accl_ref)
     accr_ref[...] = jnp.zeros_like(accr_ref)
 
-    def own_res(c, carry):
-        for n in range(4):
-            g = c * 4 + n
-            build_group(rb_ref[g], g * 128, 0, a_ref, wz_ref, (wx_ref, wy_ref))
-        spread_chunk(c * 512, 512, acc_ref, a_ref, wz_ref)
-        return carry
-
-    lax.fori_loop(0, RES // 512, own_res, 0)
+    def residents(block, x0, acc, a, wz, own):
+        for half in range(2):
+            rows = slice(half * 8, half * 8 + 8)
+            ready = prepare(
+                block[0, rows, :], [block[1 + d, rows, :] for d in range(3)], block[4, rows, :], x0
+            )
+            for s in range(8):
+                build_group(ready, s, half * 1024 + s * 128, a, wz, own)
+            spread_chunk(half * 1024, 1024, acc, a, wz)
+
+    residents(rb_ref, 0, acc_ref, a_ref, wz_ref, (wx_ref, wy_ref))
 
     for k in range(1, ny):
         hop1(k).wait()
@@ -319,16 +343,8 @@
     for copy in x_copies:
         copy.wait()
 
-    def near_res(c, carry):
-        for n in range(4):
-            g = c * 4 + n
-            build_group(rl_ref[g], g * 128, 20, al_ref, wl_ref, None)
-            build_group(rr_ref[g], g * 128, 0, ar_ref, wr_ref, None)
-        spread_chunk(c * 512, 512, accl_ref, al_ref, wl_ref)
-        spread_chunk(c * 512, 512, accr_ref, ar_ref, wr_ref)
-        return carry
-
-    lax.fori_loop(0, RES // 512, near_res, 0)
+    residents(rl_ref, 20, accl_ref, al_ref, wl_ref, None)
+    residents(rr_ref, 0, accr_ref, ar_ref, wr_ref, None)
 
     with jax.named_scope("matrices"):
         col = iota((64, 256), 1)
@@ -363,20 +379,17 @@
     for n in range(3):
         rt_ref[n] = r2_ref[:, n].reshape(nx * ny, 128).T
 
-    def all_arr(c, carry):
-        for n in range(4):
-            s = c * 4 + n
-            at = RES + s * 128
-            rows = pl.ds(pl.multiple_of(s * 8, 8), 8)
-            build_group(rt_ref[1, rows, :], at, 0, a_ref, wz_ref, (wx_ref, wy_ref))
-            build_group(rt_ref[0, rows, :], at, 20, al_ref, wl_ref, None)
-            build_group(rt_ref[2, rows, :], at, 0, ar_ref, wr_ref, None)
-        spread_chunk(RES + c * 512, 512, acc_ref, a_ref, wz_ref)
-        spread_chunk(RES + c * 512, 512, accl_ref, al_ref, wl_ref)
-        spread_chunk(RES + c * 512, 512, accr_ref, ar_ref, wr_ref)
-        return carry
-
-    lax.fori_loop(0, ARR // 512, all_arr, 0)
+    for side, x0, a, wz, own in (
+        (1, 0, a_ref, wz_ref, (wx_ref, wy_ref)),
+        (0, 20, al_ref, wl_ref, None),
+        (2, 0, ar_ref, wr_ref, None),
+    ):
+        field = [rt_ref[side, f * 8 : f * 8 + 8, :] for f in range(5)]
+        ready = prepare(field[0], field[1:4], field[4], x0)
+        for s in range(8):
+            build_group(ready, s, RES + s * 128, a, wz, own)
+    for acc, a, wz in ((acc_ref, a_ref, wz_ref), (accl_ref, al_ref, wl_ref), (accr_ref, ar_ref, wr_ref)):
+        spread_chunk(RES, ARR, acc, a, wz)
 
     up_y = lax.rem(gy + 1, ny)
     down_y = lax.rem(gy + ny - 1, ny)
@@ -539,11 +552,13 @@
         ao_ref[pl.ds(2 * c + 1, 1), :] = value[:, 128:256]
         return carry
 
-    lax.fori_loop(0, RES // 256, sample_res, 0)
+    for c in range(RES // 256):
+        sample_res(c, 0)
     outputs[1].start()
-    lax.fori_loop(0, ARR // 256, sample_arr, 0)
-
-    occupied = jnp.concatenate([rt_ref[1, s * 8 + 4 : s * 8 + 5, :] for s in range(8)], axis=0)
+    for c in range(ARR // 256):
+        sample_arr(c, 0)
+
+    occupied = rt_ref[1, 32:40, :]
     value = jnp.where(occupied > 0.5, ao_ref[...], 0.0)
     hi, mid, lo = split3(value)
     wide = (NZ, ARR)
@@ -606,9 +621,9 @@
             pltpu.VMEM((nx + 2, ny, 128), F32),
             pltpu.VMEM((nx, 3, ny, 128), F32),
             pltpu.VMEM((3, 128, 128), F32),
-            pltpu.VMEM((16, 8, 128), F32),
-            pltpu.VMEM((16, 8, 128), F32),
-            pltpu.VMEM((16, 8, 128), F32),
+            pltpu.VMEM((5, 16, 128), F32),
+            pltpu.VMEM((5, 16, 128), F32),
+            pltpu.VMEM((5, 16, 128), F32),
             pltpu.VMEM((ROWS, ATOMS), BF16),
             pltpu.VMEM((near, ATOMS), BF16),
             pltpu.VMEM((near, ATOMS), BF16),

time: 38.4 us -> 34.6 us (0.901)
  Pallas kernels: 36.4 us -> 32.7 us
    pallas_call x1, Pallas kernels: 34.7 us -> 31 us  [on_device(): pl.pallas_call(functools.partial(kernel, nx, ny), out_shape=(jax.ShapeDty...]
where the time goes in v3:
time: 34.6 us; the launch traced here: 34 us
  Pallas kernels  32.7 us (95%)
  between operations  1.29 us (4%)
    pallas_call x1, Pallas kernels, on_device(): pl.pallas_call(functools.partial(kernel, nx, ny), out_shape=(jax.ShapeDty...  31 us
    pallas_call x1, Pallas kernels, on_device(): pl.pallas_call(hand_out, out_shape=(jax.ShapeDtypeStruct((16, 128), F32),...  1.73 us

profile of v3, /device:TPU:0, one launch (start us, length us, event | category | flops | bytes accessed | tf_op | source)
XLA Modules:
  0.0 34.0 jit_solution(13498402925777998600)
XLA Ops:
  1.3 31.0 %multilevel.1 = (f32[16,128]{1,0:T(8,128)}, f32[1,1024]{1,0:T(1,128)}, f32[512,128]{1,0:T(8,128)}) custom-call(f32[16,128]{1,0:T(8,128)} %bitcast.7, f32[3,2048]{1,0:T(4,128)} %rf_hbm.1, s32[16,128]{1,0:T(8,128)} %bitcast.8, s32[1]{0:T(128)S(6)} %copy.13.count_hbm, f32[1,512]{1,0:T(1,128)} %bitcast.9, f32[3,512]{1,0:T(4,128)} %mf_hbm.1, s32[1,512]{1,0:T(1,128)} %bitcast.10, ...), custom_call_target="tpu_custom_call" | custom-call | tf_op jit(solution)/shard_map/multilevel/pallas_call | solution.py:595
  32.3 1.7 %hand_out.1 = (f32[16,128]{1,0:T(8,128)}, f32[1,1024]{1,0:T(1,128)}, f32[512,128]{1,0:T(8,128)}) custom-call(f32[16,128]{1,0:T(8,128)} %get-tuple-element.9.refs_0_, f32[1,1024]{1,0:T(1,128)} %get-tuple-element.10.refs_1_, f32[512,128]{1,0:T(8,128)} %get-tuple-element.11.refs_2_), custom_call_target="tpu_custom_call" | custom-call | tf_op jit(solution)/shard_map/hand_out/pallas_call | solution.py:681

commit v4 on v3

--- a/solution.py
+++ b/solution.py
@@ -99,7 +99,8 @@
     z = iota((NZ, 128), 0).astype(BF16)
     at_z, hi, lo = ([v.astype(BF16) for v in each] for each in (at_z, hi, lo))
     wz_ref[0:NZ, lanes] = pick(z, at_z, hi)
-    wz_ref[NZ : 2 * NZ, lanes] = pick(z, at_z, lo)
+    if own is not None:
+        wz_ref[NZ : 2 * NZ, lanes] = pick(z, at_z, lo)
     wxq = wx * charge
     for p in range(YP // 2):
         blk = jnp.concatenate(
@@ -116,7 +117,7 @@
 
 def spread_chunk(lane0, size, acc_ref, a_ref, wz_ref):
     lanes = lane_window(lane0, size)
-    acc_ref[...] += dot_nt(a_ref[:, lanes], wz_ref[:, lanes])
+    acc_ref[...] += dot_nt(a_ref[:, lanes], wz_ref[0:NZ, lanes])
 
 
 def tap_sum(t, taps_ref, dim):
@@ -205,6 +206,16 @@
     gx = lax.axis_index("gx")
     gy = lax.axis_index("gy")
 
+    barrier = pltpu.get_barrier_semaphore()
+    for k in range(1, ny):
+        pl.semaphore_signal(
+            barrier, inc=1, device_id=(gx, lax.rem(gy + k, ny)), device_id_type=MESH
+        )
+    for k in range(1, nx):
+        pl.semaphore_signal(
+            barrier, inc=1, device_id=(lax.rem(gx + k, nx), gy), device_id_type=MESH
+        )
+
     inputs = [
         pltpu.make_async_copy(src, dst, in_sem.at[n])
         for n, (src, dst) in enumerate(
@@ -225,15 +236,6 @@
     for copy in inputs:
         copy.start()
 
-    barrier = pltpu.get_barrier_semaphore()
-    for k in range(1, ny):
-        pl.semaphore_signal(
-            barrier, inc=1, device_id=(gx, lax.rem(gy + k, ny)), device_id_type=MESH
-        )
-    for k in range(1, nx):
-        pl.semaphore_signal(
-            barrier, inc=1, device_id=(lax.rem(gx + k, nx), gy), device_id_type=MESH
-        )
     for copy in inputs[:4]:
         copy.wait()
 
@@ -379,17 +381,21 @@
     for n in range(3):
         rt_ref[n] = r2_ref[:, n].reshape(nx * ny, 128).T
 
-    for side, x0, a, wz, own in (
-        (1, 0, a_ref, wz_ref, (wx_ref, wy_ref)),
-        (0, 20, al_ref, wl_ref, None),
-        (2, 0, ar_ref, wr_ref, None),
-    ):
-        field = [rt_ref[side, f * 8 : f * 8 + 8, :] for f in range(5)]
-        ready = prepare(field[0], field[1:4], field[4], x0)
-        for s in range(8):
-            build_group(ready, s, RES + s * 128, a, wz, own)
-    for acc, a, wz in ((acc_ref, a_ref, wz_ref), (accl_ref, al_ref, wl_ref), (accr_ref, ar_ref, wr_ref)):
-        spread_chunk(RES, ARR, acc, a, wz)
+    boxes = (
+        (1, 0, acc_ref, a_ref, wz_ref, (wx_ref, wy_ref)),
+        (0, 20, accl_ref, al_ref, wl_ref, None),
+        (2, 0, accr_ref, ar_ref, wr_ref, None),
+    )
+    for n in range(len(boxes) + 1):
+        if n < len(boxes):
+            side, x0, _, a, wz, own = boxes[n]
+            field = [rt_ref[side, f * 8 : f * 8 + 8, :] for f in range(5)]
+            ready = prepare(field[0], field[1:4], field[4], x0)
+        if n > 0:
+            spread_chunk(RES, ARR, *boxes[n - 1][2:5])
+        if n < len(boxes):
+            for s in range(8):
+                build_group(ready, s, RES + s * 128, a, wz, own)
 
     up_y = lax.rem(gy + 1, ny)
     down_y = lax.rem(gy + ny - 1, ny)
@@ -398,7 +404,7 @@
         rows = []
         for ref, count in ((acc_ref, XP), (accl_ref, 16), (accr_ref, 16)):
             part = ref[y * count : (y + 1) * count]
-            rows.append(part[:, 0:NZ] + part[:, NZ : 2 * NZ])
+            rows.append(part)
             if count == XP:
                 rows.append(jnp.zeros((8, NZ), F32))
         hi, lo = split2(jnp.concatenate(rows, axis=0))
@@ -439,10 +445,10 @@
         )
 
     y_copies = [
-        y_copy(0, f_ref.at[:, pl.ds(10 * NZ, FH * NZ)], fl_ref, up_y),
-        y_copy(1, f_ref.at[:, pl.ds(0, FH * NZ)], fr_ref, down_y),
-        y_copy(2, c3_ref.at[pl.ds(1, CH)], cl_ref, up_y),
-        y_copy(3, c3_ref.at[pl.ds(0, CH)], cr_ref, down_y),
+        y_copy(0, c3_ref.at[pl.ds(1, CH)], cl_ref, up_y),
+        y_copy(1, c3_ref.at[pl.ds(0, CH)], cr_ref, down_y),
+        y_copy(2, f_ref.at[:, pl.ds(10 * NZ, FH * NZ)], fl_ref, up_y),
+        y_copy(3, f_ref.at[:, pl.ds(0, FH * NZ)], fr_ref, down_y),
     ]
     for copy in y_copies:
         copy.start()
@@ -474,27 +480,12 @@
     for m in range(5):
         cin_ref[:, (2 * m + 6) * NZ : (2 * m + 8) * NZ] = own[m * CP : (m + 1) * CP]
 
-    for copy in y_copies:
+    for copy in y_copies[0:2]:
         copy.wait()
-    for ref, at in ((fl_ref, 0), (fr_ref, 22)):
-        halo = fine_z(stacked(ref, FH))
-        for y in range(FH):
-            fin_ref[:, (y + at) * NZ : (y + at + 1) * NZ] += halo[y * XP : (y + 1) * XP]
     for ref, at in ((cl_ref, 0), (cr_ref, 14)):
         halo = coarse_z(jnp.concatenate([ref[m] for m in range(CH)], axis=0))
         for m in range(CH):
             cin_ref[:, (2 * m + at) * NZ : (2 * m + at + 2) * NZ] += halo[m * CP : (m + 1) * CP]
-
-    def fine_y(i, carry):
-        rows = pl.ds(pl.multiple_of(i * 8, 8), 8)
-        out = jnp.zeros((8, YR * NZ), F32)
-        for k in range(TAPS):
-            out = out + ft_ref[1, k] * fin_ref[rows, k * NZ : (k + YR) * NZ]
-        fo_ref[rows, 0 : YR * NZ] = out
-        fo_ref[rows, YR * NZ : YP * NZ] = jnp.zeros((8, NZ), F32)
-        return carry
-
-    lax.fori_loop(0, XP // 8, fine_y, 0)
 
     def coarse_y(i, carry):
         rows = pl.ds(pl.multiple_of(i * 8, 8), 8)
@@ -509,16 +500,31 @@
 
     lax.fori_loop(0, CP // 8, coarse_y, 0)
 
+    for copy in y_copies[2:4]:
+        copy.wait()
+    for ref, at in ((fl_ref, 0), (fr_ref, 22)):
+        halo = fine_z(stacked(ref, FH))
+        for y in range(FH):
+            fin_ref[:, (y + at) * NZ : (y + at + 1) * NZ] += halo[y * XP : (y + 1) * XP]
+
+    def fine_y(i, carry):
+        rows = pl.ds(pl.multiple_of(i * 8, 8), 8)
+        out = jnp.zeros((8, YR * NZ), F32)
+        for k in range(TAPS):
+            out = out + ft_ref[1, k] * fin_ref[rows, k * NZ : (k + YR) * NZ]
+        for y in range(YR):
+            fo_ref[rows, y * NZ : (y + 1) * NZ] = (
+                out[:, y * NZ : (y + 1) * NZ] + up_ref[y // 2, rows, :]
+            )
+        fo_ref[rows, YR * NZ : YP * NZ] = jnp.zeros((8, NZ), F32)
+        return carry
+
+    lax.fori_loop(0, XP // 8, fine_y, 0)
+
     for p in range(YP // 2):
-        add = up_ref[p, 0:XP, :]
-        rows = []
-        for y in (2 * p, 2 * p + 1):
-            total = fo_ref[:, y * NZ : (y + 1) * NZ] + add
-            if y < CY:
-                for i in range(CX // 8):
-                    grid_ref[pl.ds(y + i * 8 * CY, 8, stride=CY), :] = total[i * 8 : i * 8 + 8]
-            rows.append(total)
-        half = jnp.concatenate(rows, axis=0).astype(BF16)
+        half = jnp.concatenate(
+            [fo_ref[:, y * NZ : (y + 1) * NZ] for y in (2 * p, 2 * p + 1)], axis=0
+        ).astype(BF16)
         hb_ref[p * 2 * XP : (p + 1) * 2 * XP, 0:NZ] = half
         hb_ref[p * 2 * XP : (p + 1) * 2 * XP, NZ : 2 * NZ] = half
 
@@ -527,36 +533,34 @@
         pltpu.make_async_copy(res_ref, res_hbm, out_sem.at[1]),
         pltpu.make_async_copy(arr_ref, arr_hbm, out_sem.at[2]),
     ]
-    outputs[0].start()
-
-    def sample_at(c):
-        lanes = pl.ds(pl.multiple_of(c * 256, 256), 256)
-        values = dot_nn(hb_ref[...], wz_ref[:, lanes])
+
+    def values_of(c):
+        return dot_nn(hb_ref[...], wz_ref[:, c * 256 : (c + 1) * 256])
+
+    def reduced(c, values):
+        lanes = slice(c * 256, (c + 1) * 256)
         wy = wy_ref[:, lanes]
         part = jnp.zeros((XP, 256), F32)
         for y in range(YR):
             part = part + wy[y : y + 1] * values[y * XP : (y + 1) * XP]
-        return jnp.sum(part * wx_ref[:, lanes], axis=0, keepdims=True)
-
-    def sample_res(c, carry):
-        value = sample_at(c)
-        live = iota((1, 256), 1) + c * 256 < count_ref[0]
-        value = jnp.where(live, value, 0.0)
-        res_ref[pl.ds(2 * c, 1), :] = value[:, 0:128]
-        res_ref[pl.ds(2 * c + 1, 1), :] = value[:, 128:256]
-        return carry
-
-    def sample_arr(c, carry):
-        value = sample_at(c + RES // 256)
-        ao_ref[pl.ds(2 * c, 1), :] = value[:, 0:128]
-        ao_ref[pl.ds(2 * c + 1, 1), :] = value[:, 128:256]
-        return carry
-
-    for c in range(RES // 256):
-        sample_res(c, 0)
-    outputs[1].start()
-    for c in range(ARR // 256):
-        sample_arr(c, 0)
+        value = jnp.sum(part * wx_ref[:, lanes], axis=0, keepdims=True)
+        if c < RES // 256:
+            live = iota((1, 256), 1) + c * 256 < count_ref[0]
+            value = jnp.where(live, value, 0.0)
+            at, ref = 2 * c, res_ref
+        else:
+            at, ref = 2 * (c - RES // 256), ao_ref
+        ref[at : at + 1, :] = value[:, 0:128]
+        ref[at + 1 : at + 2, :] = value[:, 128:256]
+
+    for c in range(RES // 256, ATOMS // 256):
+        reduced(c, values_of(c))
+    for y in range(CY):
+        for i in range(CX // 8):
+            grid_ref[pl.ds(y + i * 8 * CY, 8, stride=CY), :] = fo_ref[
+                i * 8 : i * 8 + 8, y * NZ : (y + 1) * NZ
+            ]
+    outputs[0].start()
 
     occupied = rt_ref[1, 32:40, :]
     value = jnp.where(occupied > 0.5, ao_ref[...], 0.0)
@@ -568,6 +572,10 @@
     keep = (iota((8, ARR), 1) & 7) == iota((8, ARR), 0)
     arr_ref[...] = jnp.sum(jnp.where(keep, flat, 0.0), axis=0, keepdims=True)
     outputs[2].start()
+
+    for c in range(RES // 256):
+        reduced(c, values_of(c))
+    outputs[1].start()
     for copy in outputs:
         copy.wait()
 
@@ -630,11 +638,11 @@
             pltpu.VMEM((XP, ATOMS), F32),
             pltpu.VMEM((CP, ATOMS), F32),
             pltpu.VMEM((2 * NZ, ATOMS), BF16),
-            pltpu.VMEM((2 * NZ, ATOMS), BF16),
-            pltpu.VMEM((2 * NZ, ATOMS), BF16),
-            pltpu.VMEM((ROWS, 2 * NZ), F32),
-            pltpu.VMEM((near, 2 * NZ), F32),
-            pltpu.VMEM((near, 2 * NZ), F32),
+            pltpu.VMEM((NZ, ATOMS), BF16),
+            pltpu.VMEM((NZ, ATOMS), BF16),
+            pltpu.VMEM((ROWS, NZ), F32),
+            pltpu.VMEM((near, NZ), F32),
+            pltpu.VMEM((near, NZ), F32),
             pltpu.VMEM((256, lanes), BF16),
             pltpu.VMEM((64, 256), BF16),
             pltpu.VMEM((2 * NZ, 2 * NZ), BF16),

time: 34.6 us -> 34 us (0.983)
  Pallas kernels: 32.7 us -> 32.1 us
    pallas_call x1, Pallas kernels: 31 us -> 30.4 us  [on_device(): pl.pallas_call(functools.partial(kernel, nx, ny), out_shape=(jax.ShapeDty...]
where the time goes in v4:
time: 34 us; the launch traced here: 33.4 us
  Pallas kernels  32.1 us (94%)
  between operations  1.29 us (4%)
    pallas_call x1, Pallas kernels, on_device(): pl.pallas_call(functools.partial(kernel, nx, ny), out_shape=(jax.ShapeDty...  30.4 us
    pallas_call x1, Pallas kernels, on_device(): pl.pallas_call(hand_out, out_shape=(jax.ShapeDtypeStruct((16, 128), F32),...  1.73 us

profile of v4, /device:TPU:0, one launch (start us, length us, event | category | flops | bytes accessed | tf_op | source)
XLA Modules:
  0.0 33.4 jit_solution(12892046237028802103)
XLA Ops:
  1.3 30.4 %multilevel.1 = (f32[16,128]{1,0:T(8,128)}, f32[1,1024]{1,0:T(1,128)}, f32[512,128]{1,0:T(8,128)}) custom-call(f32[16,128]{1,0:T(8,128)} %bitcast.7, f32[3,2048]{1,0:T(4,128)} %rf_hbm.1, s32[16,128]{1,0:T(8,128)} %bitcast.8, s32[1]{0:T(128)S(6)} %copy.13.count_hbm, f32[1,512]{1,0:T(1,128)} %bitcast.9, f32[3,512]{1,0:T(4,128)} %mf_hbm.1, s32[1,512]{1,0:T(1,128)} %bitcast.10, ...), custom_call_target="tpu_custom_call" | custom-call | tf_op jit(solution)/shard_map/multilevel/pallas_call | solution.py:603
  31.7 1.7 %hand_out.1 = (f32[16,128]{1,0:T(8,128)}, f32[1,1024]{1,0:T(1,128)}, f32[512,128]{1,0:T(8,128)}) custom-call(f32[16,128]{1,0:T(8,128)} %get-tuple-element.9.refs_0_, f32[1,1024]{1,0:T(1,128)} %get-tuple-element.10.refs_1_, f32[512,128]{1,0:T(8,128)} %get-tuple-element.11.refs_2_), custom_call_target="tpu_custom_call" | custom-call | tf_op jit(solution)/shard_map/hand_out/pallas_call | solution.py:689

commit v5 on v4

--- a/solution.py
+++ b/solution.py
@@ -186,6 +186,9 @@
     fr_ref,
     cl_ref,
     cr_ref,
+    edge_ref,
+    el_ref,
+    er_ref,
     fin_ref,
     cin_ref,
     fo_ref,
@@ -444,11 +447,20 @@
             device_id_type=MESH,
         )
 
+    for n, (y0, m0) in enumerate(((10, 1), (0, 0))):
+        for y in range(FH):
+            edge_ref[n, 3 * y : 3 * y + 3, :] = f_ref[32:35, (y0 + y) * NZ : (y0 + y + 1) * NZ]
+        edge_ref[n, 27:32, :] = jnp.zeros((5, NZ), F32)
+        for m in range(CH):
+            edge_ref[n, 32 + 2 * m : 34 + 2 * m, :] = c3_ref[m0 + m, 16:18, :]
+    whole, half = pl.ds(0, 32), pl.ds(0, 16)
     y_copies = [
-        y_copy(0, c3_ref.at[pl.ds(1, CH)], cl_ref, up_y),
-        y_copy(1, c3_ref.at[pl.ds(0, CH)], cr_ref, down_y),
-        y_copy(2, f_ref.at[:, pl.ds(10 * NZ, FH * NZ)], fl_ref, up_y),
-        y_copy(3, f_ref.at[:, pl.ds(0, FH * NZ)], fr_ref, down_y),
+        y_copy(0, edge_ref.at[0], el_ref, up_y),
+        y_copy(1, edge_ref.at[1], er_ref, down_y),
+        y_copy(2, c3_ref.at[pl.ds(1, CH), half], cl_ref, up_y),
+        y_copy(3, c3_ref.at[pl.ds(0, CH), half], cr_ref, down_y),
+        y_copy(4, f_ref.at[whole, pl.ds(10 * NZ, FH * NZ)], fl_ref, up_y),
+        y_copy(5, f_ref.at[whole, pl.ds(0, FH * NZ)], fr_ref, down_y),
     ]
     for copy in y_copies:
         copy.start()
@@ -480,12 +492,14 @@
     for m in range(5):
         cin_ref[:, (2 * m + 6) * NZ : (2 * m + 8) * NZ] = own[m * CP : (m + 1) * CP]
 
-    for copy in y_copies[0:2]:
+    for copy in y_copies[0:4]:
         copy.wait()
-    for ref, at in ((cl_ref, 0), (cr_ref, 14)):
-        halo = coarse_z(jnp.concatenate([ref[m] for m in range(CH)], axis=0))
+    for ref, edge, at in ((cl_ref, el_ref, 0), (cr_ref, er_ref, 14)):
+        halo = coarse_z(jnp.concatenate([ref[m] for m in range(CH)] + [edge[32:40, :]], axis=0))
         for m in range(CH):
-            cin_ref[:, (2 * m + at) * NZ : (2 * m + at + 2) * NZ] += halo[m * CP : (m + 1) * CP]
+            lanes = slice((2 * m + at) * NZ, (2 * m + at + 2) * NZ)
+            cin_ref[0:16, lanes] += halo[m * 16 : (m + 1) * 16]
+            cin_ref[16:18, lanes] += halo[64 + 2 * m : 66 + 2 * m]
 
     def coarse_y(i, carry):
         rows = pl.ds(pl.multiple_of(i * 8, 8), 8)
@@ -500,12 +514,14 @@
 
     lax.fori_loop(0, CP // 8, coarse_y, 0)
 
-    for copy in y_copies[2:4]:
+    for copy in y_copies[4:6]:
         copy.wait()
-    for ref, at in ((fl_ref, 0), (fr_ref, 22)):
-        halo = fine_z(stacked(ref, FH))
+    for ref, edge, at in ((fl_ref, el_ref, 0), (fr_ref, er_ref, 22)):
+        halo = fine_z(jnp.concatenate([stacked(ref, FH), edge[0:32, :]], axis=0))
         for y in range(FH):
-            fin_ref[:, (y + at) * NZ : (y + at + 1) * NZ] += halo[y * XP : (y + 1) * XP]
+            lanes = slice((y + at) * NZ, (y + at + 1) * NZ)
+            fin_ref[0:32, lanes] += halo[y * 32 : (y + 1) * 32]
+            fin_ref[32:35, lanes] += halo[288 + 3 * y : 291 + 3 * y]
 
     def fine_y(i, carry):
         rows = pl.ds(pl.multiple_of(i * 8, 8), 8)
@@ -649,10 +665,13 @@
             pltpu.VMEM((3 * NZ, 2 * NZ), BF16),
             pltpu.VMEM((XP, lanes), F32),
             pltpu.VMEM((5, CP, NZ), F32),
-            pltpu.VMEM((XP, FH * NZ), F32),
-            pltpu.VMEM((XP, FH * NZ), F32),
-            pltpu.VMEM((CH, CP, NZ), F32),
-            pltpu.VMEM((CH, CP, NZ), F32),
+            pltpu.VMEM((32, FH * NZ), F32),
+            pltpu.VMEM((32, FH * NZ), F32),
+            pltpu.VMEM((CH, 16, NZ), F32),
+            pltpu.VMEM((CH, 16, NZ), F32),
+            pltpu.VMEM((2, 40, NZ), F32),
+            pltpu.VMEM((40, NZ), F32),
+            pltpu.VMEM((40, NZ), F32),
             pltpu.VMEM((XP, 31 * NZ), F32),
             pltpu.VMEM((CP, 22 * NZ), F32),
             pltpu.VMEM((XP, YP * NZ), F32),
@@ -667,8 +686,8 @@
             dma((nx,)),
             dma((2,)),
             dma((2,)),
-            dma((4,)),
-            dma((4,)),
+            dma((6,)),
+            dma((6,)),
         ],
         compiler_params=pltpu.CompilerParams(
             collective_id=0, has_side_effects=True, vmem_limit_bytes=64 << 20

time: 34 us -> 33.4 us (0.982)
  Pallas kernels: 32.1 us -> 31.5 us
    pallas_call x1, Pallas kernels: 30.4 us -> 29.8 us  [on_device(): pl.pallas_call(functools.partial(kernel, nx, ny), out_shape=(jax.ShapeDty...]
where the time goes in v5:
time: 33.4 us; the launch traced here: 32.8 us
  Pallas kernels  31.5 us (94%)
  between operations  1.29 us (4%)
    pallas_call x1, Pallas kernels, on_device(): pl.pallas_call(functools.partial(kernel, nx, ny), out_shape=(jax.ShapeDty...  29.8 us
    pallas_call x1, Pallas kernels, on_device(): pl.pallas_call(hand_out, out_shape=(jax.ShapeDtypeStruct((16, 128), F32),...  1.73 us

profile of v5, /device:TPU:0, one launch (start us, length us, event | category | flops | bytes accessed | tf_op | source)
XLA Modules:
  0.0 32.8 jit_solution(1106685929766716109)
XLA Ops:
  1.3 29.8 %multilevel.1 = (f32[16,128]{1,0:T(8,128)}, f32[1,1024]{1,0:T(1,128)}, f32[512,128]{1,0:T(8,128)}) custom-call(f32[16,128]{1,0:T(8,128)} %bitcast.7, f32[3,2048]{1,0:T(4,128)} %rf_hbm.1, s32[16,128]{1,0:T(8,128)} %bitcast.8, s32[1]{0:T(128)S(6)} %copy.13.count_hbm, f32[1,512]{1,0:T(1,128)} %bitcast.9, f32[3,512]{1,0:T(4,128)} %mf_hbm.1, s32[1,512]{1,0:T(1,128)} %bitcast.10, ...), custom_call_target="tpu_custom_call" | custom-call | tf_op jit(solution)/shard_map/multilevel/pallas_call | solution.py:619
  31.1 1.7 %hand_out.1 = (f32[16,128]{1,0:T(8,128)}, f32[1,1024]{1,0:T(1,128)}, f32[512,128]{1,0:T(8,128)}) custom-call(f32[16,128]{1,0:T(8,128)} %get-tuple-element.9.refs_0_, f32[1,1024]{1,0:T(1,128)} %get-tuple-element.10.refs_1_, f32[512,128]{1,0:T(8,128)} %get-tuple-element.11.refs_2_), custom_call_target="tpu_custom_call" | custom-call | tf_op jit(solution)/shard_map/hand_out/pallas_call | solution.py:708

commit v6 on v5

--- a/solution.py
+++ b/solution.py
@@ -277,7 +277,7 @@
             device_id_type=MESH,
         )
 
-    for k in range(1, ny):
+    for k in far_first(ny):
         hop1(k).start()
     mine = pl.ds(pl.multiple_of(gy * nx, nx), nx)
     b1_ref[mine, :] = snd_ref[mine, :]
@@ -341,7 +341,7 @@
             device_id_type=MESH,
         )
 
-    for k in range(1, nx):
+    for k in far_first(nx):
         hop2(k).start()
     r2_ref[gx] = t2_ref[pl.ds(gx, 3)]
 
@@ -419,6 +419,33 @@
     conv = dot_nn(bx_ref[...], xh_ref[...])
     f_ref[...] = conv[0:XP]
 
+    def y_copy(n, src, dst, to):
+        return pltpu.make_async_remote_copy(
+            src_ref=src,
+            dst_ref=dst,
+            send_sem=sy_sem.at[n],
+            recv_sem=ry_sem.at[n],
+            device_id=(gx, to),
+            device_id_type=MESH,
+        )
+
+    def fine_copy(n, y0, first, count, dst, to):
+        return y_copy(
+            n,
+            f_ref.at[pl.ds(0, 32), pl.ds((y0 + first) * NZ, count * NZ)],
+            dst.at[:, pl.ds(first * NZ, count * NZ)],
+            to,
+        )
+
+    fine_copies = [
+        fine_copy(4, 10, 0, 5, fl_ref, up_y),
+        fine_copy(5, 0, 0, 5, fr_ref, down_y),
+        fine_copy(6, 10, 5, 4, fl_ref, up_y),
+        fine_copy(7, 0, 5, 4, fr_ref, down_y),
+    ]
+    for copy in fine_copies[0:2]:
+        copy.start()
+
     r, c = iota((2 * NZ, NZ), 0), iota((2 * NZ, NZ), 1)
     pair = jnp.where(lax.shift_right_logical(r, 1) == c, 1.0, 0.0).astype(BF16)
     coarse = conv[XP : XP + CP]
@@ -437,32 +464,20 @@
     for m in range(5):
         c3_ref[m] = packed[m * CP : (m + 1) * CP]
 
-    def y_copy(n, src, dst, to):
-        return pltpu.make_async_remote_copy(
-            src_ref=src,
-            dst_ref=dst,
-            send_sem=sy_sem.at[n],
-            recv_sem=ry_sem.at[n],
-            device_id=(gx, to),
-            device_id_type=MESH,
-        )
-
     for n, (y0, m0) in enumerate(((10, 1), (0, 0))):
         for y in range(FH):
             edge_ref[n, 3 * y : 3 * y + 3, :] = f_ref[32:35, (y0 + y) * NZ : (y0 + y + 1) * NZ]
         edge_ref[n, 27:32, :] = jnp.zeros((5, NZ), F32)
         for m in range(CH):
             edge_ref[n, 32 + 2 * m : 34 + 2 * m, :] = c3_ref[m0 + m, 16:18, :]
-    whole, half = pl.ds(0, 32), pl.ds(0, 16)
+    half = pl.ds(0, 16)
     y_copies = [
         y_copy(0, edge_ref.at[0], el_ref, up_y),
         y_copy(1, edge_ref.at[1], er_ref, down_y),
         y_copy(2, c3_ref.at[pl.ds(1, CH), half], cl_ref, up_y),
         y_copy(3, c3_ref.at[pl.ds(0, CH), half], cr_ref, down_y),
-        y_copy(4, f_ref.at[whole, pl.ds(10 * NZ, FH * NZ)], fl_ref, up_y),
-        y_copy(5, f_ref.at[whole, pl.ds(0, FH * NZ)], fr_ref, down_y),
     ]
-    for copy in y_copies:
+    for copy in y_copies + fine_copies[2:4]:
         copy.start()
 
     def fine_z(block):
@@ -492,7 +507,7 @@
     for m in range(5):
         cin_ref[:, (2 * m + 6) * NZ : (2 * m + 8) * NZ] = own[m * CP : (m + 1) * CP]
 
-    for copy in y_copies[0:4]:
+    for copy in y_copies:
         copy.wait()
     for ref, edge, at in ((cl_ref, el_ref, 0), (cr_ref, er_ref, 14)):
         halo = coarse_z(jnp.concatenate([ref[m] for m in range(CH)] + [edge[32:40, :]], axis=0))
@@ -514,7 +529,7 @@
 
     lax.fori_loop(0, CP // 8, coarse_y, 0)
 
-    for copy in y_copies[4:6]:
+    for copy in fine_copies:
         copy.wait()
     for ref, edge, at in ((fl_ref, el_ref, 0), (fr_ref, er_ref, 22)):
         halo = fine_z(jnp.concatenate([stacked(ref, FH), edge[0:32, :]], axis=0))
@@ -594,6 +609,11 @@
     outputs[1].start()
     for copy in outputs:
         copy.wait()
+
+
+def far_first(count):
+    turn = count // 2
+    return sorted(range(1, count), key=lambda k: (-min(k % turn, turn - k % turn), -k))
 
 
 def hand_out(*refs):
@@ -686,8 +706,8 @@
             dma((nx,)),
             dma((2,)),
             dma((2,)),
-            dma((6,)),
-            dma((6,)),
+            dma((8,)),
+            dma((8,)),
         ],
         compiler_params=pltpu.CompilerParams(
             collective_id=0, has_side_effects=True, vmem_limit_bytes=64 << 20

time: 33.4 us -> 32.7 us (0.979); the launches traced: 32.8 us -> 32.5 us
  no operation moved by 1% of the time
where the time goes in v6:
time: 32.7 us; the launch traced here: 32.5 us
  Pallas kernels  31.2 us (95%)
  between operations  1.29 us (4%)
    pallas_call x1, Pallas kernels, on_device(): pl.pallas_call(functools.partial(kernel, nx, ny), out_shape=(jax.ShapeDty...  29.5 us
    pallas_call x1, Pallas kernels, on_device(): pl.pallas_call(hand_out, out_shape=(jax.ShapeDtypeStruct((16, 128), F32),...  1.73 us

profile of v6, /device:TPU:0, one launch (start us, length us, event | category | flops | bytes accessed | tf_op | source)
XLA Modules:
  0.0 32.5 jit_solution(10977444580745594526)
XLA Ops:
  1.3 29.5 %multilevel.1 = (f32[16,128]{1,0:T(8,128)}, f32[1,1024]{1,0:T(1,128)}, f32[512,128]{1,0:T(8,128)}) custom-call(f32[16,128]{1,0:T(8,128)} %bitcast.7, f32[3,2048]{1,0:T(4,128)} %rf_hbm.1, s32[16,128]{1,0:T(8,128)} %bitcast.8, s32[1]{0:T(128)S(6)} %copy.13.count_hbm, f32[1,512]{1,0:T(1,128)} %bitcast.9, f32[3,512]{1,0:T(4,128)} %mf_hbm.1, s32[1,512]{1,0:T(1,128)} %bitcast.10, ...), custom_call_target="tpu_custom_call" | custom-call | tf_op jit(solution)/shard_map/multilevel/pallas_call | solution.py:639
  30.8 1.7 %hand_out.1 = (f32[16,128]{1,0:T(8,128)}, f32[1,1024]{1,0:T(1,128)}, f32[512,128]{1,0:T(8,128)}) custom-call(f32[16,128]{1,0:T(8,128)} %get-tuple-element.9.refs_0_, f32[1,1024]{1,0:T(1,128)} %get-tuple-element.10.refs_1_, f32[512,128]{1,0:T(8,128)} %get-tuple-element.11.refs_2_), custom_call_target="tpu_custom_call" | custom-call | tf_op jit(solution)/shard_map/hand_out/pallas_call | solution.py:728

commit v7 on v6

--- a/solution.py
+++ b/solution.py
@@ -181,6 +181,7 @@
     zf_ref,
     zc_ref,
     f_ref,
+    co_ref,
     c3_ref,
     fl_ref,
     fr_ref,
@@ -402,22 +403,23 @@
 
     up_y = lax.rem(gy + 1, ny)
     down_y = lax.rem(gy + ny - 1, ny)
-    for y in range(YR):
-        lanes = slice(y * NZ, (y + 1) * NZ)
-        rows = []
-        for ref, count in ((acc_ref, XP), (accl_ref, 16), (accr_ref, 16)):
-            part = ref[y * count : (y + 1) * count]
-            rows.append(part)
-            if count == XP:
-                rows.append(jnp.zeros((8, NZ), F32))
-        hi, lo = split2(jnp.concatenate(rows, axis=0))
-        xh_ref[0:80, lanes] = hi
-        xh_ref[80:160, lanes] = lo
-        xh_ref[160:240, lanes] = hi
-        xh_ref[240:256, lanes] = jnp.zeros((16, NZ), BF16)
-
-    conv = dot_nn(bx_ref[...], xh_ref[...])
-    f_ref[...] = conv[0:XP]
+    def x_pass(y0, y1):
+        for y in range(y0, y1):
+            lanes = slice(y * NZ, (y + 1) * NZ)
+            rows = []
+            for ref, count in ((acc_ref, XP), (accl_ref, 16), (accr_ref, 16)):
+                rows.append(ref[y * count : (y + 1) * count])
+                if count == XP:
+                    rows.append(jnp.zeros((8, NZ), F32))
+            hi, lo = split2(jnp.concatenate(rows, axis=0))
+            xh_ref[0:80, lanes] = hi
+            xh_ref[80:160, lanes] = lo
+            xh_ref[160:240, lanes] = hi
+            xh_ref[240:256, lanes] = jnp.zeros((16, NZ), BF16)
+        lanes = slice(y0 * NZ, y1 * NZ)
+        conv = dot_nn(bx_ref[...], xh_ref[:, lanes])
+        f_ref[:, lanes] = conv[0:XP]
+        co_ref[:, lanes] = conv[XP : XP + CP]
 
     def y_copy(n, src, dst, to):
         return pltpu.make_async_remote_copy(
@@ -443,12 +445,16 @@
         fine_copy(6, 10, 5, 4, fl_ref, up_y),
         fine_copy(7, 0, 5, 4, fr_ref, down_y),
     ]
-    for copy in fine_copies[0:2]:
-        copy.start()
+    x_pass(10, 15)
+    fine_copies[0].start()
+    x_pass(0, 5)
+    fine_copies[1].start()
+    x_pass(15, 19)
+    x_pass(5, 10)
 
     r, c = iota((2 * NZ, NZ), 0), iota((2 * NZ, NZ), 1)
     pair = jnp.where(lax.shift_right_logical(r, 1) == c, 1.0, 0.0).astype(BF16)
-    coarse = conv[XP : XP + CP]
+    coarse = co_ref[...]
     tiles = []
     for m in range(5):
         both = []
@@ -684,6 +690,7 @@
             pltpu.VMEM((2 * NZ, 2 * NZ), BF16),
             pltpu.VMEM((3 * NZ, 2 * NZ), BF16),
             pltpu.VMEM((XP, lanes), F32),
+            pltpu.VMEM((CP, lanes), F32),
             pltpu.VMEM((5, CP, NZ), F32),
             pltpu.VMEM((32, FH * NZ), F32),
             pltpu.VMEM((32, FH * NZ), F32),

time: 32.7 us -> 32.6 us (level)
  no operation moved by 1% of the time
where the time goes in v7:
time: 32.6 us; the launch traced here: 32.3 us
  Pallas kernels  31.1 us (95%)
  between operations  1.29 us (4%)
    pallas_call x1, Pallas kernels, on_device(): pl.pallas_call(functools.partial(kernel, nx, ny), out_shape=(jax.ShapeDty...  29.3 us
    pallas_call x1, Pallas kernels, on_device(): pl.pallas_call(hand_out, out_shape=(jax.ShapeDtypeStruct((16, 128), F32),...  1.73 us

profile of v7, /device:TPU:0, one launch (start us, length us, event | category | flops | bytes accessed | tf_op | source)
XLA Modules:
  0.0 32.3 jit_solution(10217447712020291448)
XLA Ops:
  1.3 29.3 %multilevel.1 = (f32[16,128]{1,0:T(8,128)}, f32[1,1024]{1,0:T(1,128)}, f32[512,128]{1,0:T(8,128)}) custom-call(f32[16,128]{1,0:T(8,128)} %bitcast.7, f32[3,2048]{1,0:T(4,128)} %rf_hbm.1, s32[16,128]{1,0:T(8,128)} %bitcast.8, s32[1]{0:T(128)S(6)} %copy.13.count_hbm, f32[1,512]{1,0:T(1,128)} %bitcast.9, f32[3,512]{1,0:T(4,128)} %mf_hbm.1, s32[1,512]{1,0:T(1,128)} %bitcast.10, ...), custom_call_target="tpu_custom_call" | custom-call | tf_op jit(solution)/shard_map/multilevel/pallas_call | solution.py:645
  30.6 1.7 %hand_out.1 = (f32[16,128]{1,0:T(8,128)}, f32[1,1024]{1,0:T(1,128)}, f32[512,128]{1,0:T(8,128)}) custom-call(f32[16,128]{1,0:T(8,128)} %get-tuple-element.9.refs_0_, f32[1,1024]{1,0:T(1,128)} %get-tuple-element.10.refs_1_, f32[512,128]{1,0:T(8,128)} %get-tuple-element.11.refs_2_), custom_call_target="tpu_custom_call" | custom-call | tf_op jit(solution)/shard_map/hand_out/pallas_call | solution.py:735

commit v8 on v7

--- a/solution.py
+++ b/solution.py
@@ -211,11 +211,11 @@
     gy = lax.axis_index("gy")
 
     barrier = pltpu.get_barrier_semaphore()
-    for k in range(1, ny):
+    for k in far_first(ny):
         pl.semaphore_signal(
             barrier, inc=1, device_id=(gx, lax.rem(gy + k, ny)), device_id_type=MESH
         )
-    for k in range(1, nx):
+    for k in far_first(nx):
         pl.semaphore_signal(
             barrier, inc=1, device_id=(lax.rem(gx + k, nx), gy), device_id_type=MESH
         )

time: 32.6 us -> 32.6 us (level)
  no operation moved by 1% of the time
where the time goes in v8:
time: 32.6 us; the launch traced here: 32.3 us
  Pallas kernels  31.1 us (95%)
  between operations  1.29 us (4%)
    pallas_call x1, Pallas kernels, on_device(): pl.pallas_call(functools.partial(kernel, nx, ny), out_shape=(jax.ShapeDty...  29.3 us
    pallas_call x1, Pallas kernels, on_device(): pl.pallas_call(hand_out, out_shape=(jax.ShapeDtypeStruct((16, 128), F32),...  1.73 us

profile of v8, /device:TPU:0, one launch (start us, length us, event | category | flops | bytes accessed | tf_op | source)
XLA Modules:
  0.0 32.3 jit_solution(7558909222643863504)
XLA Ops:
  1.3 29.3 %multilevel.1 = (f32[16,128]{1,0:T(8,128)}, f32[1,1024]{1,0:T(1,128)}, f32[512,128]{1,0:T(8,128)}) custom-call(f32[16,128]{1,0:T(8,128)} %bitcast.7, f32[3,2048]{1,0:T(4,128)} %rf_hbm.1, s32[16,128]{1,0:T(8,128)} %bitcast.8, s32[1]{0:T(128)S(6)} %copy.13.count_hbm, f32[1,512]{1,0:T(1,128)} %bitcast.9, f32[3,512]{1,0:T(4,128)} %mf_hbm.1, s32[1,512]{1,0:T(1,128)} %bitcast.10, ...), custom_call_target="tpu_custom_call" | custom-call | tf_op jit(solution)/shard_map/multilevel/pallas_call | solution.py:645
  30.6 1.7 %hand_out.1 = (f32[16,128]{1,0:T(8,128)}, f32[1,1024]{1,0:T(1,128)}, f32[512,128]{1,0:T(8,128)}) custom-call(f32[16,128]{1,0:T(8,128)} %get-tuple-element.9.refs_0_, f32[1,1024]{1,0:T(1,128)} %get-tuple-element.10.refs_1_, f32[512,128]{1,0:T(8,128)} %get-tuple-element.11.refs_2_), custom_call_target="tpu_custom_call" | custom-call | tf_op jit(solution)/shard_map/hand_out/pallas_call | solution.py:735
